TPU v7x, 512 devices: a whole 4x4x16 slice. The times are simulated.
512 devices in a mesh: grp: 16 (over x_lo, y, core), tok: 32 (over x_hi, z).
Axes of the slice: x: 4 (x_hi: 2, x_lo: 2; x = x_hi * 2 + x_lo), y: 4, z: 16, core: 2. Of those that a mesh axis runs over, the one named last changes fastest.
Arguments:
- probe_states: bfloat16 [1024, 2048], P('tok'), may hold values from -40 to 40
- norm_gain: float32 [2048], replicated, may hold values from 0.1 to 1.9
- gate_weight: bfloat16 [98304, 2048], P(('grp', 'tok')), may hold values from -1 to 1
- up_weight: bfloat16 [98304, 2048], P(('grp', 'tok')), may hold values from -1 to 1
- down_weight: bfloat16 [98304, 2048], P(('grp', 'tok')), may hold values from -1 to 1
- route_weight: float32 [512, 256], P(('grp', 'tok')), may hold values from 0.02 to 1
Outputs:
- features: bfloat16 [131072, 2048], P(('grp', 'tok'))
- cka: float32 [128, 128], replicated
All inputs are finite; a program needn't handle non-finite values.
Results may differ from a plain program's by a relative error of at most 0.0015.
The roundings to bfloat16 on the way count: a program that leaves them out, or rounds other values in their place, can miss the bound.
Values may be sent and summed in bfloat16 or wider, within the bound.
A program may use at most 64 MiB of HBM per device.

v0:
```python
import jax
import jax.numpy as jnp
from jax import lax
from jax.sharding import PartitionSpec as P


def swapped(array, axis, bit):
    return lax.ppermute(array, axis, [(i, i ^ 1 << bit) for i in range(lax.axis_size(axis))])


def shards(probe_states, norm_gain, gate_weight, up_weight, down_weight, route_weight):
    contract = (((1,), (1,)), ((), ()))
    states = probe_states.astype(jnp.float32)
    scaled = (
        states * lax.rsqrt(jnp.mean(states * states, axis=1, keepdims=True) + 1e-06) * norm_gain
    )
    normed = scaled.astype(jnp.bfloat16)
    position = lax.axis_index("tok")
    route_column = route_weight[0][:, None]
    piece = lax.all_gather(normed, "tok", axis=0, tiled=True)
    gate = lax.dot_general(piece, gate_weight, contract, preferred_element_type=jnp.float32)
    upward = lax.dot_general(piece, up_weight, contract, preferred_element_type=jnp.float32)
    gathered = jnp.dot(
        (jax.nn.silu(gate) * upward).astype(jnp.bfloat16),
        down_weight,
        preferred_element_type=jnp.float32,
    )
    current = gathered
    for bit_number in (1, 0):
        bit_value = position >> bit_number & 1
        half_rows = current.shape[0] // 2
        kept_part = lax.dynamic_slice_in_dim(current, bit_value * half_rows, half_rows, 0)
        sent_part = lax.dynamic_slice_in_dim(current, (1 - bit_value) * half_rows, half_rows, 0)
        current = kept_part + swapped(sent_part, "tok", bit_number)
    features = (current * route_column).astype(jnp.bfloat16)
    every_row = features
    for bit_number in (0, 1):
        bit_value = position >> bit_number & 1
        got_rows = swapped(every_row, "tok", bit_number)
        every_row = jnp.where(
            bit_value == 0,
            jnp.concatenate([every_row, got_rows], 0),
            jnp.concatenate([got_rows, every_row], 0),
        )
    token_count = every_row.shape[0]
    column_mean = jnp.sum(every_row, axis=0, dtype=jnp.float32) / token_count
    projection_all = jnp.sum(every_row.astype(jnp.float32) * column_mean, axis=1)
    projection_own = jnp.sum(features.astype(jnp.float32) * column_mean, axis=1)
    mean_square = jnp.sum(column_mean * column_mean)
    gram = lax.dot_general(features, every_row, contract, preferred_element_type=jnp.float32)
    centered = (gram - projection_own[:, None] - projection_all[None, :] + mean_square).astype(
        jnp.bfloat16
    )
    group_count = lax.axis_size("grp")
    token_devices = lax.axis_size("tok")
    blocks = centered.reshape(group_count, token_devices, -1)
    arrived = lax.all_to_all(
        lax.all_to_all(blocks, "grp", split_axis=0, concat_axis=0, tiled=True),
        "tok",
        split_axis=1,
        concat_axis=1,
        tiled=True,
    )
    flat = arrived.reshape(group_count * token_devices // 4, -1)
    partial_value = lax.dot_general(flat, flat, contract, preferred_element_type=jnp.float32)
    pair_totals = lax.psum(partial_value, ("grp", "tok"))
    diagonal = jnp.diagonal(pair_totals)
    cka = pair_totals / jnp.sqrt(diagonal[:, None] * diagonal[None, :])
    return (features, cka)


def solution(mesh):
    return jax.shard_map(
        shards,
        mesh=mesh,
        in_specs=(
            P("tok", None),
            P(),
            P(("grp", "tok"), None),
            P(("grp", "tok"), None),
            P(("grp", "tok"), None),
            P(("grp", "tok"), None),
        ),
        out_specs=(P(("grp", "tok"), None), P()),
        check_vma=False,
    )
```

profile of v0, /device:TPU:1, one launch (start us, length us, event | category | flops | bytes accessed | tf_op | source)
XLA Modules:
  0.0 1075.3 jit_solution(5629643619523636164)
XLA Ops:
  8.4 1.7 fusion.14
  10.1 161.1 %all-gather.2.cloned.1.call-done = bf16[1024,2048]{1,0:T(8,128)(2,1)} async-done(((bf16[32,2048]{1,0:T(8,128)(2,1)}), bf16[1024,2048]{1,0:T(8,128)(2,1)}) %all-gather.2.cloned.1.call-update) | async-done | bytes 4194320 | tf_op jit(solution)/shard_map/all_gather | solution.py:20
  171.2 3.9 fusion.16
  175.2 8.1 fusion.5
  183.3 4.6 constant_dynamic-slice_fusion.1
  187.9 3.2 collective-permute-start
  191.1 181.4 %collective-permute-done = f32[512,2048]{1,0:T(8,128)} collective-permute-done((f32[512,2048]{1,0:T(8,128)}, f32[512,2048]{1,0:T(8,128)}, u32[]{:S(2)}, u32[]{:S(2)}) %collective-permute-start) | collective-permute-done | bytes 4194336 | tf_op jit(solution)/shard_map/ppermute | solution.py:8
  372.6 4.2 dynamic-slice_add_fusion
  376.8 1.9 copy-done.1
  380.2 1.9 collective-permute-start.1
  382.1 46.0 %collective-permute-done.1 = f32[256,2048]{1,0:T(8,128)S(1)} collective-permute-done((f32[256,2048]{1,0:T(8,128)}, f32[256,2048]{1,0:T(8,128)S(1)}, u32[]{:S(2)}, u32[]{:S(2)}) %collective-permute-start.1) | collective-permute-done | bytes 2097184 | tf_op jit(solution)/shard_map/ppermute | solution.py:8
  429.5 2.4 multiply_convert_fusion
  431.9 2.2 collective-permute-start.2
  434.2 22.3 %collective-permute-done.2 = bf16[256,2048]{1,0:T(8,128)(2,1)} collective-permute-done((bf16[256,2048]{1,0:T(8,128)(2,1)S(1)}, bf16[256,2048]{1,0:T(8,128)(2,1)}, u32[]{:S(2)}, u32[]{:S(2)}) %collective-permute-start.2) | collective-permute-done | bytes 1048608 | tf_op jit(solution)/shard_map/ppermute | solution.py:8
  456.5 3.1 maximum_select_fusion.1
  459.6 4.1 collective-permute-start.3
  463.8 90.7 %collective-permute-done.3 = bf16[512,2048]{1,0:T(8,128)(2,1)} collective-permute-done((bf16[512,2048]{1,0:T(8,128)(2,1)S(1)}, bf16[512,2048]{1,0:T(8,128)(2,1)}, u32[]{:S(2)}, u32[]{:S(2)}) %collective-permute-start.3) | collective-permute-done | bytes 2097184 | tf_op jit(solution)/shard_map/ppermute | solution.py:8
  554.5 2.9 convert_reduce_fusion
  558.3 3.1 fusion
  561.4 4.3 fusion.3
  565.9 14.8 %all_to_all.10 = bf16[16,32,512]{2,1,0:T(8,128)(2,1)S(1)} all-to-all(bf16[16,32,512]{2,1,0:T(8,128)(2,1)S(1)} %reshape.27), channel_id=1, replica_groups=mesh['grp'=16,'tok'=32] {'grp'}, dimensions={0} | all-to-all | bytes 1048576 | tf_op jit(solution)/shard_map/all_to_all | solution.py:58
  580.9 41.5 %all_to_all.11 = bf16[16,32,512]{2,0,1:T(8,128)(2,1)S(1)} all-to-all(bf16[16,32,512]{2,0,1:T(8,128)(2,1)S(1)} %copy.11), channel_id=1, replica_groups=mesh['grp'=16,'tok'=32] {'tok'}, dimensions={1} | all-to-all | bytes 1048576 | tf_op jit(solution)/shard_map/all_to_all | solution.py:57
  624.0 440.9 %all-reduce.2.cloned.1.call-done = f32[128,128]{1,0:T(8,128)} async-done(((f32[128,128]{1,0:T(8,128)}), f32[128,128]{1,0:T(8,128)}) %all-reduce.2.cloned.1.call-update) | async-done | bytes 65552 | tf_op jit(solution)/shard_map/psum | solution.py:66
  1064.9 1.9 gather_fusion
  (29 shorter events, 8.6 us)
Async XLA Ops:
  7.2 168.0 %copy-start = (bf16[192,2048]{1,0:T(8,128)(2,1)S(1)}, bf16[192,2048]{1,0:T(8,128)(2,1)}, u32[]{:S(2)}) copy-start(bf16[192,2048]{1,0:T(8,128)(2,1)} %param.10) | copy-start | bytes 2359300
  7.2 168.0 %copy-start.5 = (bf16[192,2048]{1,0:T(8,128)(2,1)S(1)}, bf16[192,2048]{1,0:T(8,128)(2,1)}, u32[]{:S(2)}) copy-start(bf16[192,2048]{1,0:T(8,128)(2,1)} %param.9) | copy-start | bytes 2359300
  7.2 164.1 %all-gather.2.cloned.1.call-start = ((), (), s32[]{:S(2)}) async-start(), calls=%async_computation.2 | async-start | bytes 4325376 | tf_op jit(solution)/shard_map/all_gather | solution.py:20
  10.1 1054.8 %all-reduce.2.cloned.1.call-start = ((), (), s32[]{:S(2)}) async-start(), calls=%async_computation.3 | async-start | bytes 131072 | tf_op jit(solution)/shard_map/psum | solution.py:66
  187.9 184.6 %collective-permute-start = (f32[512,2048]{1,0:T(8,128)}, f32[512,2048]{1,0:T(8,128)}, u32[]{:S(2)}, u32[]{:S(2)}) collective-permute-start(f32[512,2048]{1,0:T(8,128)} %constant_dynamic-slice_fusion.1), channel_id=1, source_target_pairs={{0,2},{1,3},{2,0},{3,1},{4,6},{5,7},{6,4},{7,5},{8,10},{9,11},{10,... | collective-permute-start | bytes 12582920 | tf_op jit(solution)/shard_map/ppermute | solution.py:8
  376.8 1.9 copy-start.1
  378.7 50.7 %copy-start.6 = (f32[1,256]{1,0:T(1,128)S(1)}, f32[1,256]{1,0:T(1,128)}, u32[]{:S(2)}) copy-start(f32[1,256]{1,0:T(1,128)} %param.11) | copy-start | bytes 3076
  380.2 47.9 %collective-permute-start.1 = (f32[256,2048]{1,0:T(8,128)}, f32[256,2048]{1,0:T(8,128)S(1)}, u32[]{:S(2)}, u32[]{:S(2)}) collective-permute-start(f32[256,2048]{1,0:T(8,128)} %constant_dynamic-slice_fusion), channel_id=1, source_target_pairs={{0,1},{1,0},{2,3},{3,2},{4,5},{5,4},{6,7},{7,6},{8,9},{9,8},{10,11... | collective-permute-start | bytes 6291464 | tf_op jit(solution)/shard_map/ppermute | solution.py:8
  428.1 1.3 copy-start.4
  431.9 2.2 copy-start.2
  431.9 24.5 %collective-permute-start.2 = (bf16[256,2048]{1,0:T(8,128)(2,1)S(1)}, bf16[256,2048]{1,0:T(8,128)(2,1)}, u32[]{:S(2)}, u32[]{:S(2)}) collective-permute-start(bf16[256,2048]{1,0:T(8,128)(2,1)S(1)} %multiply_convert_fusion), channel_id=1, source_target_pairs={{0,1},{1,0},{2,3},{3,2},{4,5},{5,4},{6,7},{7,6},{8,9},{9,8},{10,11... | collective-permute-start | bytes 3145736 | tf_op jit(solution)/shard_map/ppermute | solution.py:8
  459.6 94.9 %collective-permute-start.3 = (bf16[512,2048]{1,0:T(8,128)(2,1)S(1)}, bf16[512,2048]{1,0:T(8,128)(2,1)}, u32[]{:S(2)}, u32[]{:S(2)}) collective-permute-start(bf16[512,2048]{1,0:T(8,128)(2,1)S(1)} %maximum_select_fusion.1), channel_id=1, source_target_pairs={{0,2},{1,3},{2,0},{3,1},{4,6},{5,7},{6,4},{7,5},{8,10},{9,11},{10,... | collective-permute-start | bytes 6291464 | tf_op jit(solution)/shard_map/ppermute | solution.py:8
  463.7 94.2 %copy-start.3 = (bf16[256,2048]{1,0:T(8,128)(2,1)S(1)}, bf16[256,2048]{1,0:T(8,128)(2,1)}, u32[]{:S(2)}) copy-start(bf16[256,2048]{1,0:T(8,128)(2,1)} %copy-done.2) | copy-start | bytes 3145732
Sparse Core Ops, SparseCore 0:
  11.7 159.5 all-gather.1
  624.1 440.7 all-reduce.1
where the time goes:
time: 1080 us
  waiting for transfers between devices  943 us (87%)
  blocking collectives  56.3 us (5%)
  other arithmetic  21.1 us (2%)
  matrix products  17.2 us (2%)
  between operations  14.2 us (1%)
  local copies, waits for them, and re-layouts  12.4 us (1%)
  starting transfers between devices  11.5 us (1%)
    psum x1, waiting for transfers between devices, shards(): pair_totals = lax.psum(partial_value, ('grp', 'tok'))  441 us
    ppermute x4, waiting for transfers between devices, swapped(): lax.ppermute(array, axis, [(i, i ^ 1 << bit) for i in range(lax.axis_size...  340 us
    all_gather x1, waiting for transfers between devices, shards(): piece = lax.all_gather(normed, 'tok', axis=0, tiled=True)  161 us
    all_to_all x1, blocking collectives, shards(): lax.all_to_all(lax.all_to_all(blocks, 'grp', split_axis=0, concat_axis=0,...  41.5 us
  transfers between devices with their start and end apart: 6, of which 6 were waited for; matrix products, arithmetic and copies ran while one was open for 0% of the time, Pallas kernels for 0%

commit v1 on v0

v1 whole, which is shorter than its diff:
```python
import functools

import jax
import jax.numpy as jnp
from jax import lax
from jax.experimental import pallas as pl
from jax.experimental.pallas import tpu as pltpu
from jax.sharding import PartitionSpec as P

F32 = jnp.float32
BF16 = jnp.bfloat16
NT = (((1,), (1,)), ((), ()))
MESH = pl.DeviceIdType.MESH
VM = pl.BlockSpec(memory_space=pltpu.VMEM)


class Place:
    def __init__(self):
        self.g = lax.axis_index("grp")
        self.t = lax.axis_index("tok")
        self.xl = self.g // 8
        self.y = (self.g // 2) % 4
        self.c = self.g % 2
        self.xh = self.t // 16
        self.z = self.t % 16
        self.q = self.t % 4
        self.h = self.t // 4
        self.base = self.h * 4
        self.owner_q = 1 + self.c
        self.owner = self.base + self.owner_q
        self.rank = (self.q + 4 - self.owner_q) % 4

    def at_y(self, step):
        return (self.xl * 8 + ((self.y + step) % 4) * 2 + self.c, self.t)

    def at_x(self, step):
        x = (self.xh * 2 + self.xl + step) % 4
        return ((x % 2) * 8 + self.y * 2 + self.c, (x // 2) * 16 + self.z)

    def at_z(self, step):
        return (self.g, self.xh * 16 + (self.z + step) % 16)

    def at_core(self):
        return (self.xl * 8 + self.y * 2 + 1 - self.c, self.t)


def push(src, dst, send, recv, device):
    return pltpu.make_async_remote_copy(
        src_ref=src, dst_ref=dst, send_sem=send, recv_sem=recv, device_id=device, device_id_type=MESH
    )


def greet(devices):
    barrier = pltpu.get_barrier_semaphore()
    for device in devices:
        pl.semaphore_signal(barrier, inc=1, device_id=device, device_id_type=MESH)
    return barrier


def expert_kernel(
    x_ref, gain_ref, gate_ref, up_ref, down_ref, route_ref,
    feat_ref,
    nrm, tok, hid, downs, routes,
    z_send, z_recv, y_send, y_recv, x_send, x_recv, c_send, c_recv, w_send, w_recv, d_send, d_recv,
):
    me = Place()
    partners = [me.at_z(s) for s in range(1, 16)]
    partners += [me.at_x(1), me.at_x(3), me.at_y(1), me.at_y(3), me.at_core()]
    barrier = greet(partners)

    states = x_ref[...].astype(F32)
    scale = lax.rsqrt(jnp.mean(states * states, axis=1, keepdims=True) + 1e-06)
    nrm[...] = (states * scale * gain_ref[...]).astype(BF16)
    group = me.c * 8 + me.xl * 4 + me.y
    rows = pl.ds(pl.multiple_of(me.t * 32, 32), 32)
    columns = pl.ds(pl.multiple_of(group * 128, 128), 128)
    tok[rows, columns] = nrm[:, columns]
    pl.semaphore_wait(barrier, len(partners))

    sends = []

    def start(copy):
        copy.start()
        sends.append(copy)

    for s in range(1, 16):
        start(push(nrm.at[:, columns], tok.at[rows, columns], z_send.at[s], z_recv.at[s], me.at_z(s)))
    for s in range(1, 16):
        source = pl.ds(pl.multiple_of((me.xh * 16 + (me.z + 16 - s) % 16) * 32, 32), 32)
        push(nrm.at[:, columns], tok.at[source, columns], z_send.at[s], z_recv.at[s], me.at_z(s)).wait_recv()

    def spot(step_x, y):
        x = (me.xh * 2 + me.xl + step_x) % 4
        row = pl.multiple_of((x // 2) * 512, 512)
        return row, pl.multiple_of((me.c * 8 + (x % 2) * 4 + y) * 128, 128)

    def y_copy(part, direction, source_step, slot):
        row, col = spot(0, (me.y + source_step) % 4)
        start_row, count = ((0, 512), (0, 256), (256, 256))[part]
        block = tok.at[pl.ds(row + start_row, count), pl.ds(col, 128)]
        return push(block, block, y_send.at[slot], y_recv.at[slot], me.at_y(direction))

    def x_copy(slot, direction, source_step, y):
        row, col = spot(source_step, y)
        block = tok.at[pl.ds(row, 512), pl.ds(col, 128)]
        return push(block, block, x_send.at[slot, y], x_recv.at[slot, y], me.at_x(direction))

    def core_copy(step_x, core):
        x = (me.xh * 2 + me.xl + step_x) % 4
        row = pl.multiple_of((x // 2) * 512, 512)
        col = pl.multiple_of((core * 8 + (x % 2) * 4) * 128, 128)
        block = tok.at[pl.ds(row, 512), pl.ds(col, 512)]
        return push(block, block, c_send.at[step_x], c_recv.at[step_x], me.at_core())

    start(y_copy(0, 1, 0, 0))
    start(y_copy(0, 3, 0, 1))
    start(x_copy(0, 1, 0, me.y))
    start(x_copy(1, 3, 0, me.y))

    owner = (me.g, me.owner)
    slot = (me.rank + 3) % 4
    is_owner = me.rank == 0
    down_copy = push(down_ref, downs.at[slot], w_send.at[0], w_recv.at[slot, 0], owner)
    route_copy = push(route_ref, routes.at[me.q], w_send.at[1], w_recv.at[slot, 1], owner)

    @pl.when(jnp.logical_not(is_owner))
    def _():
        down_copy.start()
        route_copy.start()

    y_copy(0, 1, 3, 0).wait_recv()
    start(y_copy(1, 1, 3, 2))
    start(x_copy(0, 1, 0, (me.y + 3) % 4))
    start(x_copy(1, 3, 0, (me.y + 3) % 4))
    y_copy(0, 3, 1, 1).wait_recv()
    start(y_copy(2, 3, 1, 3))
    start(x_copy(0, 1, 0, (me.y + 1) % 4))
    start(x_copy(1, 3, 0, (me.y + 1) % 4))
    y_copy(1, 1, 2, 2).wait_recv()
    y_copy(2, 3, 2, 3).wait_recv()
    start(x_copy(0, 1, 0, (me.y + 2) % 4))
    start(x_copy(1, 3, 0, (me.y + 2) % 4))
    start(core_copy(0, me.c))

    for d in (0, 3, 1, 2):
        y = (me.y + d) % 4
        x_copy(0, 1, 3, y).wait_recv()
        x_copy(1, 3, 1, y).wait_recv()
        source = 3 - 2 * (y // 2)
        start(x_copy(2, 4 - source, source, y))
    start(core_copy(1, me.c))
    start(core_copy(3, me.c))

    def chunk_rows(k):
        block = (me.xh * 2 + k) % 4
        return block, pl.ds(pl.multiple_of(block * 256, 256), 256)

    def hidden_copy(k, source_slot):
        _, rows_k = chunk_rows(k)
        return push(
            hid.at[0, rows_k], hid.at[source_slot, rows_k], d_send.at[k], d_recv.at[source_slot, k], owner
        )

    def make_hidden(k):
        _, rows_k = chunk_rows(k)
        block = tok[rows_k, :]
        gate = lax.dot_general(block, gate_ref[...], NT, preferred_element_type=F32)
        upward = lax.dot_general(block, up_ref[...], NT, preferred_element_type=F32)
        hid[0, rows_k, :] = (gate / (1.0 + jnp.exp(-gate)) * upward).astype(BF16)

        @pl.when(jnp.logical_not(is_owner))
        def _():
            hidden_copy(k, me.rank).start()

    core_copy(0, 1 - me.c).wait_recv()
    core_copy(1 + 2 * me.xl, 1 - me.c).wait_recv()

    @pl.loop(0, 2)
    def _(k):
        make_hidden(k)

    for d in (0, 3, 1, 2):
        y = (me.y + d) % 4
        x_copy(2, 1, 2, y).wait_recv()
    start(core_copy(2, me.c))
    core_copy(3 - 2 * me.xl, 1 - me.c).wait_recv()
    core_copy(2, 1 - me.c).wait_recv()

    @pl.loop(2, 4)
    def _(k):
        make_hidden(k)

    @pl.when(is_owner)
    def _():
        for j in range(1, 4):
            device = (me.g, me.base + (me.owner_q + j) % 4)
            push(down_ref, downs.at[j - 1], w_send.at[0], w_recv.at[j - 1, 0], device).wait_recv()
            push(
                route_ref, routes.at[(me.owner_q + j) % 4], w_send.at[1], w_recv.at[j - 1, 1], device
            ).wait_recv()
        routes[me.q] = route_ref[...]

        @pl.loop(0, 4)
        def _(k):
            block, rows_k = chunk_rows(k)
            for j in range(1, 4):
                hidden_copy(k, j).wait_recv()
            route = routes[block]
            route_column = jnp.transpose(jnp.concatenate([route] * 16, axis=0))

            @pl.loop(0, 4)
            def _(n):
                cols = pl.ds(pl.multiple_of(n * 512, 512), 512)
                out = jnp.dot(hid[0, rows_k, :], down_ref[:, cols], preferred_element_type=F32)
                for j in range(1, 4):
                    out += jnp.dot(hid[j, rows_k, :], downs[j - 1, :, cols], preferred_element_type=F32)
                wide = jnp.concatenate([route_column] * 4, axis=1)
                feat_ref[rows_k, cols] = (out * wide).astype(BF16)

    @pl.when(jnp.logical_not(is_owner))
    def _():
        down_copy.wait_send()
        route_copy.wait_send()

        @pl.loop(0, 4)
        def _(k):
            hidden_copy(k, me.rank).wait_send()

    for copy in sends:
        copy.wait_send()


def make_features(probe_states, norm_gain, gate_weight, up_weight, down_weight, route_weight):
    dma = pltpu.SemaphoreType.DMA
    return pl.pallas_call(
        expert_kernel,
        out_shape=jax.ShapeDtypeStruct((1024, 2048), BF16),
        in_specs=[VM] * 6,
        out_specs=VM,
        scratch_shapes=[
            pltpu.VMEM((32, 2048), BF16),
            pltpu.VMEM((1024, 2048), BF16),
            pltpu.VMEM((4, 1024, 192), BF16),
            pltpu.VMEM((3, 192, 2048), BF16),
            pltpu.VMEM((4, 8, 256), F32),
            dma((16,)), dma((16,)), dma((4,)), dma((4,)), dma((3, 4)), dma((3, 4)),
            dma((4,)), dma((4,)), dma((2,)), dma((3, 2)), dma((4,)), dma((4, 4)),
        ],
        compiler_params=pltpu.CompilerParams(
            collective_id=0, has_side_effects=True, vmem_limit_bytes=48 << 20
        ),
        name="features",
    )(
        probe_states, norm_gain[None, :], gate_weight, up_weight, down_weight,
        jnp.broadcast_to(route_weight, (8, 256)),
    )


def exchange_kernel(cen_ref, out_ref, mid, a_send, a_recv, b_send, b_recv, local):
    me = Place()
    is_owner = me.rank == 0

    def over_grp(step):
        g = (me.g + step) % 16
        return g, (g, me.base + 1 + g % 2)

    def over_tok(step):
        h = (me.h + step) % 8
        return h, (me.g, h * 4 + me.owner_q)

    @pl.when(is_owner)
    def _():
        barrier = greet([over_grp(s)[1] for s in range(1, 16)] + [over_tok(s)[1] for s in range(1, 8)])
        pl.semaphore_wait(barrier, 22)

        def first(g_to, g_from, step, device):
            src = cen_ref.at[pl.ds(pl.multiple_of(g_to * 16, 16), 16), :]
            return push(src, mid.at[g_from], a_send.at[step], a_recv.at[step], device)

        def second(h_to, h_from, step, device):
            r = pl.ds(pl.multiple_of((h_to // 4) * 8, 8), 8)
            k = pl.ds(pl.multiple_of((h_to % 4) * 640, 128), 640)
            return push(mid.at[:, r, k], out_ref.at[:, h_from], b_send.at[step], b_recv.at[step], device)

        for s in range(1, 16):
            g, device = over_grp(s)
            first(g, me.g, s, device).start()
        mid[me.g] = cen_ref[pl.ds(pl.multiple_of(me.g * 16, 16), 16), :]
        for s in range(1, 16):
            g, device = over_grp(16 - s)
            first(me.g, g, s, device).wait_recv()
        for s in range(1, 8):
            h, device = over_tok(s)
            second(h, me.h, s, device).start()
        r = pl.ds(pl.multiple_of((me.h // 4) * 8, 8), 8)
        k = pl.ds(pl.multiple_of((me.h % 4) * 640, 128), 640)
        keep = pltpu.make_async_copy(mid.at[:, r, k], out_ref.at[:, me.h], local)
        keep.start()
        keep.wait()
        for s in range(1, 8):
            h, device = over_tok(8 - s)
            second(me.h, h, s, device).wait_recv()
        for s in range(1, 16):
            g, device = over_grp(s)
            first(g, me.g, s, device).wait_send()
        for s in range(1, 8):
            h, device = over_tok(s)
            second(h, me.h, s, device).wait_send()


def exchange(centered):
    dma = pltpu.SemaphoreType.DMA
    return pl.pallas_call(
        exchange_kernel,
        out_shape=jax.ShapeDtypeStruct((16, 8, 8, 640), BF16),
        in_specs=[VM],
        out_specs=VM,
        scratch_shapes=[
            pltpu.VMEM((16, 16, 2560), BF16),
            dma((16,)), dma((16,)), dma((8,)), dma((8,)), dma,
        ],
        compiler_params=pltpu.CompilerParams(collective_id=1, has_side_effects=True),
        name="exchange",
    )(centered)


def reduce_kernel(part_ref, feat_ref, total_ref, out_ref, first, mine, second, rows, f_send, f_recv,
                  a_send, a_recv, b_send, b_recv, c_send, c_recv):
    me = Place()
    is_owner = me.rank == 0

    def owner_of(g):
        return (g, me.base + 1 + g % 2)

    def over_tok(step):
        return (me.g, (me.t + step) % 32)

    def over_grp(step):
        return ((me.g + step) % 16, me.t)

    def in_quad(j):
        q = (me.owner_q + j) % 4
        return q, (me.g, me.base + q)

    barrier = greet([over_tok(s) for s in range(1, 32)] + [over_grp(s) for s in range(1, 16)])

    @pl.when(is_owner)
    def _():
        for s in range(1, 16, 2):
            pl.semaphore_signal(barrier, inc=1, device_id=owner_of((me.g + s) % 16), device_id_type=MESH)
        pl.semaphore_wait(barrier, 54)

    @pl.when(jnp.logical_not(is_owner))
    def _():
        pl.semaphore_wait(barrier, 46)

    def feature_copy(j):
        q, device = in_quad(j)
        src = feat_ref.at[pl.ds(pl.multiple_of(q * 256, 256), 256), :]
        return push(src, out_ref, f_send.at[j], f_recv, device)

    def a_copy(g_to, slot, device):
        src = part_ref.at[pl.ds(pl.multiple_of(g_to * 8, 8), 8), :]
        return push(src, first.at[slot], a_send.at[slot], a_recv.at[slot], device)

    @pl.when(is_owner)
    def _():
        for s in range(1, 16):
            g = (me.g + s) % 16
            a_copy(g, s, owner_of(g)).start()
        for j in range(1, 4):
            feature_copy(j).start()
        own = part_ref[pl.ds(pl.multiple_of(me.g * 8, 8), 8), :]
        for s in range(1, 16):
            a_copy(me.g, s, owner_of((me.g + 16 - s) % 16)).wait_recv()
            own += first[s]
        mine[...] = own
        second[me.h] = own

        @pl.loop(1, 32)
        def _(s):
            push(mine, second.at[me.h], b_send.at[s], b_recv.at[me.h], over_tok(s)).start()

    for h in range(8):
        source = (me.g, h * 4 + me.owner_q)

        @pl.when(source[1] != me.t)
        def _():
            push(mine, second.at[h], b_send.at[0], b_recv.at[h], source).wait_recv()

    total = second[0]
    for h in range(1, 8):
        total += second[h]
    rows[...] = total
    here = pl.ds(pl.multiple_of(me.g * 8, 8), 8)
    total_ref[here, :] = total
    for s in range(1, 16):
        push(rows, total_ref.at[here], c_send.at[s], c_recv.at[s], over_grp(s)).start()
    for s in range(1, 16):
        there = pl.ds(pl.multiple_of(((me.g + 16 - s) % 16) * 8, 8), 8)
        push(rows, total_ref.at[there], c_send.at[s], c_recv.at[s], over_grp(16 - s)).wait_recv()
    for s in range(1, 16):
        push(rows, total_ref.at[here], c_send.at[s], c_recv.at[s], over_grp(s)).wait_send()

    @pl.when(is_owner)
    def _():
        out_ref[...] = feat_ref[pl.ds(pl.multiple_of(me.q * 256, 256), 256), :]
        for s in range(1, 16):
            g = (me.g + s) % 16
            a_copy(g, s, owner_of(g)).wait_send()

        @pl.loop(1, 32)
        def _(s):
            push(mine, second.at[me.h], b_send.at[s], b_recv.at[me.h], over_tok(s)).wait_send()

        for j in range(1, 4):
            feature_copy(j).wait_send()

    @pl.when(jnp.logical_not(is_owner))
    def _():
        push(feat_ref.at[pl.ds(0, 256), :], out_ref, f_send.at[0], f_recv, (me.g, me.owner)).wait_recv()


def finish(partial, features):
    dma = pltpu.SemaphoreType.DMA
    return pl.pallas_call(
        reduce_kernel,
        out_shape=(
            jax.ShapeDtypeStruct((128, 128), F32),
            jax.ShapeDtypeStruct((256, 2048), BF16),
        ),
        in_specs=[VM, VM],
        out_specs=(VM, VM),
        scratch_shapes=[
            pltpu.VMEM((16, 8, 128), F32),
            pltpu.VMEM((8, 128), F32),
            pltpu.VMEM((8, 8, 128), F32),
            pltpu.VMEM((8, 128), F32),
            dma((4,)), dma, dma((16,)), dma((16,)), dma((32,)), dma((8,)), dma((16,)), dma((16,)),
        ],
        compiler_params=pltpu.CompilerParams(collective_id=2, has_side_effects=True),
        name="finish",
    )(partial, features)


def centered_blocks(feats):
    wide = feats.astype(F32)
    mean = jnp.sum(wide, axis=0) / 1024
    projection = jnp.sum(wide * mean, axis=1)
    mean_square = jnp.sum(mean * mean)
    pieces = [feats[256 * i : 256 * i + 256] for i in range(4)]
    parts = [projection[256 * i : 256 * i + 256] for i in range(4)]
    diagonal, upper = [], []
    for i in range(4):
        right = feats[256 * i :]
        gram = lax.dot_general(pieces[i], right, NT, preferred_element_type=F32)
        block = gram - parts[i][:, None] - projection[256 * i :][None, :] + mean_square
        block = block.astype(BF16)
        diagonal.append(block[:, :256])
        if i < 3:
            upper.append(block[:, 256:])
    return jnp.concatenate(diagonal + upper, axis=1)


def shards(probe_states, norm_gain, gate_weight, up_weight, down_weight, route_weight):
    feats = make_features(probe_states, norm_gain, gate_weight, up_weight, down_weight, route_weight)
    arrived = exchange(centered_blocks(feats))
    column = (lax.axis_index("tok") // 4 % 4) * 640 + lax.broadcasted_iota(jnp.int32, (1, 1, 1, 640), 3)
    weight = jnp.where(column < 1024, 1.0, 2.0).astype(BF16)
    left = (arrived * weight).reshape(128, -1)
    partial = lax.dot_general(left, arrived.reshape(128, -1), NT, preferred_element_type=F32)
    pair_totals, features = finish(partial, feats)
    diagonal = jnp.diagonal(pair_totals)
    cka = pair_totals / jnp.sqrt(diagonal[:, None] * diagonal[None, :])
    return (features, cka)


def solution(mesh):
    return jax.shard_map(
        shards,
        mesh=mesh,
        in_specs=(
            P("tok", None),
            P(),
            P(("grp", "tok"), None),
            P(("grp", "tok"), None),
            P(("grp", "tok"), None),
            P(("grp", "tok"), None),
        ),
        out_specs=(P(("grp", "tok"), None), P()),
        check_vma=False,
    )
```

time: 1080 us -> 179 us (0.17)
  waiting for transfers between devices: 943 us -> 0 us
  Pallas kernels: 0 us -> 150 us
  blocking collectives: 56.3 us -> 0 us
  other arithmetic: 21.1 us -> 7.49 us
  between operations: 14.2 us -> 0.85 us
  starting transfers between devices: 11.5 us -> 0 us
    psum x1 -> x0, waiting for transfers between devices: 441 us -> none  [shards(): pair_totals = lax.psum(partial_value, ('grp', 'tok'))]
    ppermute x4 -> x0, waiting for transfers between devices: 340 us -> none  [swapped(): lax.ppermute(array, axis, [(i, i ^ 1 << bit) for i in range(lax.axis_size...]
    all_gather x1 -> x0, waiting for transfers between devices: 161 us -> none  [shards(): piece = lax.all_gather(normed, 'tok', axis=0, tiled=True)]
    pallas_call x0 -> x3, Pallas kernels: none -> 150 us  [the longest x1 88.9 us: finish(): pl.pallas_call(reduce_kernel, out_shape=(jax.ShapeDtypeStruct((128, 128),...]
    all_to_all x2 -> x0, blocking collectives: 56.3 us -> none  [the longest x1 41.5 us: shards(): lax.all_to_all(lax.all_to_all(blocks, 'grp', split_axis=0, concat_axis=0,...]
    ppermute x4 -> x0, starting transfers between devices: 11.4 us -> none  [swapped(): lax.ppermute(array, axis, [(i, i ^ 1 << bit) for i in range(lax.axis_size...]
  transfers between devices with their start and end apart: 6 -> 0, of which waited for: 6 -> 0; matrix products, arithmetic and copies ran while one was open for 0% -> 0% of each run, Pallas kernels for 0% -> 0%
where the time goes in v1:
time: 179 us; the launch traced here: 178 us
  Pallas kernels  150 us (84%)
  local copies, waits for them, and re-layouts  12.6 us (7%)
  other arithmetic  7.49 us (4%)
  matrix products  7.25 us (4%)
    pallas_call x1, Pallas kernels, finish(): pl.pallas_call(reduce_kernel, out_shape=(jax.ShapeDtypeStruct((128, 128),...  88.9 us
    pallas_call x1, Pallas kernels, make_features(): pl.pallas_call(expert_kernel, out_shape=jax.ShapeDtypeStruct((1024, 2048)...  57.3 us
    unnamed x24, local copies, waits for them, and re-layouts  9.96 us
    dot_general x4, matrix products, centered_blocks(): gram = lax.dot_general(pieces[i], right, NT, preferred_element_type=F32)  6.11 us

profile of v1, /device:TPU:1, one launch (start us, length us, event | category | flops | bytes accessed | tf_op | source)
XLA Modules:
  0.0 177.9 jit_solution(4494113992959585084)
XLA Ops:
  0.6 0.7 broadcast_in_dim.18.route_ref
  1.3 1.1 copy-done
  2.4 1.1 copy-done.1
  3.6 1.1 copy-done.2
  4.7 0.9 copy-done.3
  5.6 0.7 copy-done.4
  6.3 57.3 %features.1.feat_ref = bf16[1024,2048]{1,0:T(8,128)(2,1)} custom-call(bf16[32,2048]{1,0:T(8,128)(2,1)S(1)} %copy-done.3, f32[1,2048]{1,0:T(1,128)S(1)} %bitcast.14, bf16[192,2048]{1,0:T(8,128)(2,1)S(1)} %copy-done, bf16[192,2048]{1,0:T(8,128)(2,1)S(1)} %copy-done.1, bf16[192,2048]{1,0:T(8,128)(2,1)S(1)} %copy-done.2, f32[8,256]{1,0:T(8,128)S(1)} %broadcast_in_dim.18.route_ref), custom_call_target="tpu_custom_call" | custom-call | tf_op jit(solution)/shard_map/features/pallas_call | solution.py:235
  63.6 3.0 %convert_reduce_fusion = f32[2048]{0:T(1024)S(1)} fusion(bf16[1024,2048]{1,0:T(8,128)(2,1)} %features.1.feat_ref), kind=kLoop, calls=%fused_computation.2 | loop fusion | flops 4192256 | bytes 4202496 | tf_op jit(solution)/shard_map/reduce_sum | solution.py:448
  66.6 0.6 broadcast_multiply_fusion
  67.2 0.9 fusion
  68.2 1.7 fusion.17
  69.8 1.9 %fusion.7 = bf16[256,1024]{1,0:T(8,128)(2,1)S(1)} fusion(bf16[1024,2048]{1,0:T(8,128)(2,1)S(1)} %copy-done.5, f32[]{:T(128)} %get-tuple-element.7, f32[1024]{0:T(1024)S(1)} %fusion, f32[256]{0:T(256)S(1)} %get-tuple-element.11), kind=kOutput, calls=%fused_computation.12 | convolution fusion | flops 1074790400 | bytes 5772292 | tf_op jit(solution)/shard_map/dot_general | solution.py:456
  71.8 1.4 fusion.29
  73.2 1.1 fusion.35
  74.5 1.1 copy-done.7
  75.5 3.5 %exchange.1 = bf16[16,8,8,640]{3,2,1,0:T(8,128)(2,1)} custom-call(bf16[256,2560]{1,0:T(8,128)(2,1)} %copy-done.7), custom_call_target="tpu_custom_call" | custom-call | tf_op jit(solution)/shard_map/exchange/pallas_call | solution.py:313
  79.1 1.4 multiply_bitcast_fusion
  80.6 0.2 copy.11
  80.8 1.1 copy-done.6
  82.1 1.1 fusion.41.part_ref
  83.2 88.9 %finish.1 = (f32[128,128]{1,0:T(8,128)}, bf16[256,2048]{1,0:T(8,128)(2,1)}) custom-call(f32[128,128]{1,0:T(8,128)} %fusion.41.part_ref, bf16[1024,2048]{1,0:T(8,128)(2,1)} %features.1.feat_ref), custom_call_target="tpu_custom_call" | custom-call | tf_op jit(solution)/shard_map/finish/pallas_call | solution.py:426
  172.1 1.9 %gather_fusion = f32[128]{0:T(128)S(1)} fusion(f32[128,128]{1,0:T(8,128)} %get-tuple-element.5, s32[128]{0:T(128)S(1)} %or_bitcast_fusion), kind=kCustom, calls=%fused_computation | custom fusion | bytes 2048 | tf_op jit(solution)/shard_map/jit(diagonal)/cond/branch_0_fun/gather | solution.py:473
  174.0 1.6 rsqrt_multiply_fusion
  175.6 2.3 %copy.20 = bf16[256,2048]{1,0:T(8,128)(2,1)} copy(bf16[256,2048]{1,0:T(8,128)(2,1)} %get-tuple-element.14) | data formatting | bytes 2097152
  (21 shorter events, 0.4 us)
Async XLA Ops:
  1.3 1.1 copy-start
  2.4 1.1 copy-start.1
  3.6 1.1 copy-start.2
  4.7 0.9 copy-start.3
  5.6 0.7 copy-start.4
  63.6 3.6 %copy-start.5 = (bf16[1024,2048]{1,0:T(8,128)(2,1)S(1)}, bf16[1024,2048]{1,0:T(8,128)(2,1)}, u32[]{:S(2)}) copy-start(bf16[1024,2048]{1,0:T(8,128)(2,1)} %features.1.feat_ref) | copy-start | bytes 12582916
  74.5 1.1 copy-start.7
  80.6 1.3 copy-start.6

commit v2 on v1

v2 whole, which is shorter than its diff:
```python
import functools

import jax
import jax.numpy as jnp
from jax import lax
from jax.experimental import pallas as pl
from jax.experimental.pallas import tpu as pltpu
from jax.sharding import PartitionSpec as P

F32 = jnp.float32
BF16 = jnp.bfloat16
NT = (((1,), (1,)), ((), ()))
MESH = pl.DeviceIdType.MESH
VM = pl.BlockSpec(memory_space=pltpu.VMEM)


class Place:
    def __init__(self):
        self.g = lax.axis_index("grp")
        self.t = lax.axis_index("tok")
        self.xl = self.g // 8
        self.y = (self.g // 2) % 4
        self.c = self.g % 2
        self.xh = self.t // 16
        self.z = self.t % 16
        self.q = self.t % 4
        self.h = self.t // 4
        self.base = self.h * 4
        self.owner_q = 1 + self.c
        self.owner = self.base + self.owner_q
        self.rank = (self.q + 4 - self.owner_q) % 4

    def at_y(self, step):
        return (self.xl * 8 + ((self.y + step) % 4) * 2 + self.c, self.t)

    def at_x(self, step):
        x = (self.xh * 2 + self.xl + step) % 4
        return ((x % 2) * 8 + self.y * 2 + self.c, (x // 2) * 16 + self.z)

    def at_z(self, step):
        return (self.g, self.xh * 16 + (self.z + step) % 16)

    def at_core(self):
        return (self.xl * 8 + self.y * 2 + 1 - self.c, self.t)


def push(src, dst, send, recv, device):
    return pltpu.make_async_remote_copy(
        src_ref=src, dst_ref=dst, send_sem=send, recv_sem=recv, device_id=device, device_id_type=MESH
    )


def greet(devices):
    barrier = pltpu.get_barrier_semaphore()
    for device in devices:
        pl.semaphore_signal(barrier, inc=1, device_id=device, device_id_type=MESH)
    return barrier


def cka_kernel(
    x_hbm, gain_ref, gate_hbm, up_hbm, down_hbm, route_ref,
    out_ref, cka_ref,
    x_ref, gate_ref, up_ref, down_ref, wide_route, nrm, tok, hid, downs, routes,
    feats, column_sum, proj_column, proj_row, cen, mid, arr, folded, part, first, mine, second, rows_sum, total_ref,
    l_sem, z_send, z_recv, y_send, y_recv, x_send, x_recv, c_send, c_recv, w_send, w_recv, d_send, d_recv,
    f_send, f_recv, a_send, a_recv, b_send, b_recv, k_sem, p_send, p_recv, s_send, s_recv, t_send, t_recv,
):
    me = Place()
    is_owner = me.rank == 0
    not_owner = jnp.logical_not(is_owner)

    loads = [
        pltpu.make_async_copy(src, dst, l_sem.at[i])
        for i, (src, dst) in enumerate(
            ((x_hbm, x_ref), (down_hbm, down_ref), (gate_hbm, gate_ref), (up_hbm, up_ref))
        )
    ]
    for load in loads:
        load.start()

    def over_tok(step):
        return (me.g, (me.t + step) % 32)

    def over_grp(step):
        return ((me.g + step) % 16, me.t)

    def owner_in_grp(step):
        g = (me.g + step) % 16
        return g, (g, me.base + 1 + g % 2)

    def owner_in_tok(step):
        h = (me.h + step) % 8
        return h, (me.g, h * 4 + me.owner_q)

    partners = [over_tok(s) for s in range(1, 32)] + [over_grp(s) for s in range(1, 16)]
    partners += [me.at_x(3 - 2 * me.xl)]
    barrier = greet(partners)

    @pl.when(is_owner)
    def _():
        for s in range(1, 16, 2):
            pl.semaphore_signal(barrier, inc=1, device_id=owner_in_grp(s)[1], device_id_type=MESH)

    loads[0].wait()
    states = x_ref[...].astype(F32)
    scale = lax.rsqrt(jnp.mean(states * states, axis=1, keepdims=True) + 1e-06)
    nrm[...] = (states * scale * gain_ref[...]).astype(BF16)
    wide_route[...] = jnp.broadcast_to(route_ref[...], (8, 256))
    group = me.c * 8 + me.xl * 4 + me.y
    rows = pl.ds(pl.multiple_of(me.t * 32, 32), 32)
    columns = pl.ds(pl.multiple_of(group * 128, 128), 128)
    tok[rows, columns] = nrm[:, columns]
    loads[1].wait()

    @pl.when(is_owner)
    def _():
        pl.semaphore_wait(barrier, len(partners) + 8)

    @pl.when(not_owner)
    def _():
        pl.semaphore_wait(barrier, len(partners))

    sends = []

    def start(copy):
        copy.start()
        sends.append(copy)

    for s in range(1, 16):
        start(push(nrm.at[:, columns], tok.at[rows, columns], z_send.at[s], z_recv.at[s], me.at_z(s)))
    for s in range(1, 16):
        source = pl.ds(pl.multiple_of((me.xh * 16 + (me.z + 16 - s) % 16) * 32, 32), 32)
        push(nrm.at[:, columns], tok.at[source, columns], z_send.at[s], z_recv.at[s], me.at_z(s)).wait_recv()

    def spot(step_x, y):
        x = (me.xh * 2 + me.xl + step_x) % 4
        row = pl.multiple_of((x // 2) * 512, 512)
        return row, pl.multiple_of((me.c * 8 + (x % 2) * 4 + y) * 128, 128)

    def y_copy(part, direction, source_step, slot):
        row, col = spot(0, (me.y + source_step) % 4)
        start_row, count = ((0, 512), (0, 256), (256, 256))[part]
        block = tok.at[pl.ds(row + start_row, count), pl.ds(col, 128)]
        return push(block, block, y_send.at[slot], y_recv.at[slot], me.at_y(direction))

    def x_copy(slot, direction, source_step, y):
        row, col = spot(source_step, y)
        block = tok.at[pl.ds(row, 512), pl.ds(col, 128)]
        return push(block, block, x_send.at[slot, y], x_recv.at[slot, y], me.at_x(direction))

    def core_copy(step_x, core):
        x = (me.xh * 2 + me.xl + step_x) % 4
        row = pl.multiple_of((x // 2) * 512, 512)
        col = pl.multiple_of((core * 8 + (x % 2) * 4) * 128, 128)
        block = tok.at[pl.ds(row, 512), pl.ds(col, 512)]
        return push(block, block, c_send.at[step_x], c_recv.at[step_x], me.at_core())

    start(y_copy(0, 1, 0, 0))
    start(y_copy(0, 3, 0, 1))
    start(x_copy(0, 1, 0, me.y))
    start(x_copy(1, 3, 0, me.y))

    owner = (me.g, me.owner)
    slot = (me.rank + 3) % 4
    down_copy = push(down_ref, downs.at[slot], w_send.at[0], w_recv.at[slot, 0], owner)
    route_copy = push(wide_route, routes.at[me.q], w_send.at[1], w_recv.at[slot, 1], owner)

    @pl.when(not_owner)
    def _():
        down_copy.start()
        route_copy.start()

    y_copy(0, 1, 3, 0).wait_recv()
    start(y_copy(1, 1, 3, 2))
    start(x_copy(0, 1, 0, (me.y + 3) % 4))
    start(x_copy(1, 3, 0, (me.y + 3) % 4))
    y_copy(0, 3, 1, 1).wait_recv()
    start(y_copy(2, 3, 1, 3))
    start(x_copy(0, 1, 0, (me.y + 1) % 4))
    start(x_copy(1, 3, 0, (me.y + 1) % 4))
    y_copy(1, 1, 2, 2).wait_recv()
    y_copy(2, 3, 2, 3).wait_recv()
    start(x_copy(0, 1, 0, (me.y + 2) % 4))
    start(x_copy(1, 3, 0, (me.y + 2) % 4))
    start(core_copy(0, me.c))

    for d in (0, 3, 1, 2):
        y = (me.y + d) % 4
        x_copy(0, 1, 3, y).wait_recv()
        x_copy(1, 3, 1, y).wait_recv()
        source = 3 - 2 * (y // 2)
        start(x_copy(2, 4 - source, source, y))
    start(core_copy(1, me.c))
    start(core_copy(3, me.c))

    def chunk_rows(k):
        block = (me.xh * 2 + k) % 4
        return block, pl.ds(pl.multiple_of(block * 256, 256), 256)

    def hidden_copy(k, source_slot):
        _, rows_k = chunk_rows(k)
        return push(
            hid.at[0, rows_k], hid.at[source_slot, rows_k], d_send.at[k], d_recv.at[source_slot, k], owner
        )

    def make_hidden(k):
        _, rows_k = chunk_rows(k)
        block = tok[rows_k, :]
        gate = lax.dot_general(block, gate_ref[...], NT, preferred_element_type=F32)
        upward = lax.dot_general(block, up_ref[...], NT, preferred_element_type=F32)
        hid[0, rows_k, :] = (gate / (1.0 + jnp.exp(-gate)) * upward).astype(BF16)

        @pl.when(not_owner)
        def _():
            hidden_copy(k, me.rank).start()

    loads[2].wait()
    loads[3].wait()
    core_copy(0, 1 - me.c).wait_recv()
    core_copy(1 + 2 * me.xl, 1 - me.c).wait_recv()

    @pl.loop(0, 2)
    def _(k):
        make_hidden(k)

    for d in (0, 3, 1, 2):
        y = (me.y + d) % 4
        x_copy(2, 1, 2, y).wait_recv()
    start(core_copy(2, me.c))
    core_copy(3 - 2 * me.xl, 1 - me.c).wait_recv()
    core_copy(2, 1 - me.c).wait_recv()

    @pl.loop(2, 4)
    def _(k):
        make_hidden(k)

    def feature_copy(k):
        block, rows_k = chunk_rows(k)
        return block, push(feats.at[rows_k, :], out_ref, f_send.at[k], f_recv, (me.g, me.base + block))

    def ship(k):
        block, copy = feature_copy(k)

        @pl.when(block != me.q)
        def _():
            copy.start()

    def first_copy(g_to, g_from, step, device):
        src = cen.at[pl.ds(pl.multiple_of(g_to * 16, 16), 16), :]
        return push(src, mid.at[g_from], a_send.at[step], a_recv.at[step], device)

    def slot_of(h):
        return (
            pl.ds(pl.multiple_of((h // 4) * 8, 8), 8),
            pl.ds(pl.multiple_of((h % 4) * 640, 128), 640),
        )

    def landing(g, h):
        return arr.at[pl.ds(pl.multiple_of((g * 8 + h) * 8, 8), 8), :]

    def many(step, device):
        block = arr.at[pl.ds(0, 128), :]
        return push(block, block, b_send.at[step], b_recv.at[step], device)

    def send_on(g):
        for s in range(1, 8):
            h, device = owner_in_tok(s)
            r, k = slot_of(h)
            push(mid.at[g, r, k], landing(g, me.h), b_send.at[s], b_recv.at[s], device).start()
        r, k = slot_of(me.h)
        pltpu.make_async_copy(mid.at[g, r, k], landing(g, me.h), k_sem).start()

    def part_copy(step):
        g, device = owner_in_grp(step)
        src = part.at[pl.ds(pl.multiple_of(g * 8, 8), 8), :]
        return push(src, first.at[step], p_send.at[step], p_recv.at[step], device)

    def row_copy(step):
        return push(mine, second.at[me.h], s_send.at[step], s_recv.at[me.h], over_tok(step))

    @pl.when(is_owner)
    def _():
        for j in range(1, 4):
            device = (me.g, me.base + (me.owner_q + j) % 4)
            push(down_ref, downs.at[j - 1], w_send.at[0], w_recv.at[j - 1, 0], device).wait_recv()
            push(
                wide_route, routes.at[(me.owner_q + j) % 4], w_send.at[1], w_recv.at[j - 1, 1], device
            ).wait_recv()
        routes[me.q] = wide_route[...]
        column_sum[...] = jnp.zeros_like(column_sum)

        @pl.loop(0, 4)
        def _(k):
            block, rows_k = chunk_rows(k)
            for j in range(1, 4):
                hidden_copy(k, j).wait_recv()

            @pl.when(k > 0)
            def _():
                ship(k - 1)

            route = routes[block]
            route_column = jnp.transpose(jnp.concatenate([route] * 16, axis=0))

            @pl.loop(0, 4)
            def _(n):
                cols = pl.ds(pl.multiple_of(n * 512, 512), 512)
                out = jnp.dot(hid[0, rows_k, :], down_ref[:, cols], preferred_element_type=F32)
                for j in range(1, 4):
                    out += jnp.dot(hid[j, rows_k, :], downs[j - 1, :, cols], preferred_element_type=F32)
                wide = jnp.concatenate([route_column] * 4, axis=1)
                rounded = (out * wide).astype(BF16)
                feats[rows_k, cols] = rounded
                column_sum[:, cols] += jnp.sum(rounded.astype(F32).reshape(32, 8, 512), axis=0)

        mean = jnp.sum(column_sum[...], axis=0, keepdims=True) / 1024
        mean_square = jnp.sum(mean * mean, axis=1, keepdims=True)
        column_sum[...] = jnp.broadcast_to(mean, (8, 2048))

        @pl.loop(0, 4)
        def _(i):
            rows_i = pl.ds(pl.multiple_of(i * 256, 256), 256)
            total = jnp.zeros((256, 128), F32)
            for n in range(16):
                lanes = slice(n * 128, n * 128 + 128)
                total += feats[rows_i, lanes].astype(F32) * column_sum[0:1, lanes]
            projection = jnp.broadcast_to(jnp.sum(total, axis=1, keepdims=True), (256, 128))
            proj_column[rows_i, :] = projection
            proj_row[:, rows_i] = jnp.transpose(projection)[0:8, :]

        ship(3)

        @pl.loop(0, 10)
        def _(p):
            i = p % 4
            j = (i + p // 4) % 4
            rows_i = pl.ds(pl.multiple_of(i * 256, 256), 256)
            rows_j = pl.ds(pl.multiple_of(j * 256, 256), 256)
            gram = lax.dot_general(feats[rows_i, :], feats[rows_j, :], NT, preferred_element_type=F32)
            column = proj_column[rows_i, :]
            block = gram - jnp.concatenate([column, column], axis=1) - proj_row[0:1, rows_j] + mean_square
            cen[:, pl.ds(pl.multiple_of(p * 256, 256), 256)] = block.astype(BF16)

        mid[me.g] = cen[pl.ds(pl.multiple_of(me.g * 16, 16), 16), :]
        for s in range(1, 16):
            g, device = owner_in_grp(s)
            first_copy(g, me.g, s, device).start()
        send_on(me.g)

        @pl.loop(1, 16)
        def _(s):
            g, device = owner_in_grp(16 - s)
            first_copy(me.g, g, s, device).wait_recv()
            send_on(g)

        whole = arr.at[pl.ds(0, 128), :]
        pltpu.make_async_copy(whole, whole, k_sem).wait()
        for s in range(1, 8):
            many(s, owner_in_tok(s)[1]).wait_recv()

        position = (me.h % 4) * 640 + lax.broadcasted_iota(jnp.int32, (1, 640), 1)
        weight = jnp.where(position < 1024, 1.0, 2.0)
        lane = lax.broadcasted_iota(jnp.int32, (256, 256), 1) % 8
        sublane = lax.broadcasted_iota(jnp.int32, (256, 256), 0) % 8

        @pl.loop(0, 4)
        def _(i):
            rows_i = pl.ds(pl.multiple_of(i * 256, 256), 256)
            left = (arr[rows_i, :].astype(F32) * weight).astype(BF16)

            @pl.loop(0, 4)
            def _(j):
                rows_j = pl.ds(pl.multiple_of(j * 256, 256), 256)
                block = lax.dot_general(left, arr[rows_j, :], NT, preferred_element_type=F32)
                block = jnp.where(lane == sublane, block, 0.0)
                folded[pl.ds(pl.multiple_of(i * 32, 32), 32), rows_j] = jnp.sum(block.reshape(32, 8, 256), axis=1)

        pick = lax.broadcasted_iota(jnp.int32, (1024, 128), 0) // 8
        pick = (pick == lax.broadcasted_iota(jnp.int32, (1024, 128), 1)).astype(F32).astype(BF16)
        rest = folded[...]
        result = jnp.zeros((128, 128), F32)
        for _ in range(3):
            top = rest.astype(BF16)
            rest = rest - top.astype(F32)
            result += jnp.dot(top, pick, preferred_element_type=F32)
        part[...] = result

        for s in range(1, 16):
            part_copy(s).start()
        own = part[pl.ds(pl.multiple_of(me.g * 8, 8), 8), :]
        for s in range(1, 16):
            part_copy(s).wait_recv()
            own += first[s]
        mine[...] = own
        second[me.h] = own

        @pl.loop(1, 32)
        def _(s):
            row_copy(s).start()

    for h in range(8):
        source = (me.g, h * 4 + me.owner_q)

        @pl.when(source[1] != me.t)
        def _():
            push(mine, second.at[h], s_send.at[0], s_recv.at[h], source).wait_recv()

    total = second[0]
    for h in range(1, 8):
        total += second[h]
    rows_sum[...] = total

    def total_copy(step, source):
        there = pl.ds(pl.multiple_of(source * 8, 8), 8)
        return push(rows_sum, total_ref.at[there], t_send.at[step], t_recv.at[step], over_grp(step))

    total_ref[pl.ds(pl.multiple_of(me.g * 8, 8), 8), :] = total
    for s in range(1, 16):
        total_copy(s, me.g).start()
    for s in range(1, 16):
        total_copy(s, (me.g + 16 - s) % 16).wait_recv()

    pairs = total_ref[...]
    eye = lax.broadcasted_iota(jnp.int32, (128, 128), 0) == lax.broadcasted_iota(jnp.int32, (128, 128), 1)
    only = jnp.where(eye, pairs, 0.0)
    down = jnp.sum(only, axis=1, keepdims=True)
    across = jnp.sum(only, axis=0, keepdims=True)
    cka_ref[...] = pairs / jnp.sqrt(down * across)

    for s in range(1, 16):
        total_copy(s, me.g).wait_send()

    @pl.when(is_owner)
    def _():
        out_ref[...] = feats[pl.ds(pl.multiple_of(me.q * 256, 256), 256), :]
        for s in range(1, 16):
            g, device = owner_in_grp(s)
            first_copy(g, me.g, s, device).wait_send()
            part_copy(s).wait_send()
        for s in range(1, 8):
            many(s, owner_in_tok(s)[1]).wait_send()

        @pl.loop(1, 32)
        def _(s):
            row_copy(s).wait_send()

        @pl.loop(0, 4)
        def _(k):
            block, copy = feature_copy(k)

            @pl.when(block != me.q)
            def _():
                copy.wait_send()

    @pl.when(not_owner)
    def _():
        down_copy.wait_send()
        route_copy.wait_send()

        @pl.loop(0, 4)
        def _(k):
            hidden_copy(k, me.rank).wait_send()

        push(feats.at[pl.ds(0, 256), :], out_ref, f_send.at[0], f_recv, owner).wait_recv()

    for copy in sends:
        copy.wait_send()


def shards(probe_states, norm_gain, gate_weight, up_weight, down_weight, route_weight):
    dma = pltpu.SemaphoreType.DMA
    hbm = pl.BlockSpec(memory_space=pl.ANY)
    return pl.pallas_call(
        cka_kernel,
        out_shape=(
            jax.ShapeDtypeStruct((256, 2048), BF16),
            jax.ShapeDtypeStruct((128, 128), F32),
        ),
        in_specs=[hbm, VM, hbm, hbm, hbm, VM],
        out_specs=(VM, VM),
        scratch_shapes=[
            pltpu.VMEM((32, 2048), BF16),
            pltpu.VMEM((192, 2048), BF16),
            pltpu.VMEM((192, 2048), BF16),
            pltpu.VMEM((192, 2048), BF16),
            pltpu.VMEM((8, 256), F32),
            pltpu.VMEM((32, 2048), BF16),
            pltpu.VMEM((1024, 2048), BF16),
            pltpu.VMEM((4, 1024, 192), BF16),
            pltpu.VMEM((3, 192, 2048), BF16),
            pltpu.VMEM((4, 8, 256), F32),
            pltpu.VMEM((1024, 2048), BF16),
            pltpu.VMEM((8, 2048), F32),
            pltpu.VMEM((1024, 128), F32),
            pltpu.VMEM((8, 1024), F32),
            pltpu.VMEM((256, 2560), BF16),
            pltpu.VMEM((16, 16, 2560), BF16),
            pltpu.VMEM((1024, 640), BF16),
            pltpu.VMEM((128, 1024), F32),
            pltpu.VMEM((128, 128), F32),
            pltpu.VMEM((16, 8, 128), F32),
            pltpu.VMEM((8, 128), F32),
            pltpu.VMEM((8, 8, 128), F32),
            pltpu.VMEM((8, 128), F32),
            pltpu.VMEM((128, 128), F32),
            dma((4,)), dma((16,)), dma((16,)), dma((4,)), dma((4,)), dma((3, 4)), dma((3, 4)),
            dma((4,)), dma((4,)), dma((2,)), dma((3, 2)), dma((4,)), dma((4, 4)),
            dma((4,)), dma, dma((16,)), dma((16,)), dma((8,)), dma((8,)), dma,
            dma((16,)), dma((16,)), dma((32,)), dma((8,)), dma((16,)), dma((16,)),
        ],
        compiler_params=pltpu.CompilerParams(
            collective_id=0, has_side_effects=True, vmem_limit_bytes=56 << 20
        ),
        name="cka",
    )(probe_states, norm_gain[None, :], gate_weight, up_weight, down_weight, route_weight)


def solution(mesh):
    return jax.shard_map(
        shards,
        mesh=mesh,
        in_specs=(
            P("tok", None),
            P(),
            P(("grp", "tok"), None),
            P(("grp", "tok"), None),
            P(("grp", "tok"), None),
            P(("grp", "tok"), None),
        ),
        out_specs=(P(("grp", "tok"), None), P()),
        check_vma=False,
    )
```

time: 179 us -> 144 us (0.80)
  Pallas kernels: 150 us -> 140 us
  local copies, waits for them, and re-layouts: 12.6 us -> 2.97 us
  other arithmetic: 7.49 us -> 0 us
  matrix products: 7.25 us -> 0 us
    pallas_call x3 -> x1, Pallas kernels: 150 us -> 140 us  [shards(): pl.pallas_call(cka_kernel, out_shape=(jax.ShapeDtypeStruct((256, 2048), B...]
    dot_general x5 -> x0, matrix products: 7.25 us -> none  [the longest x4 6.11 us: centered_blocks(): gram = lax.dot_general(pieces[i], right, NT, preferred_element_type=F32)]
    unnamed x24 -> x4, local copies, waits for them, and re-layouts: 9.96 us -> 2.97 us
    reduce_sum x2 -> x0, other arithmetic: 3.87 us -> none  [the longest x1 2.98 us: centered_blocks(): mean = jnp.sum(wide, axis=0) / 1024]
    div x2 -> x0, other arithmetic: 2.17 us -> none  [the longest x1 1.56 us: shards(): cka = pair_totals / jnp.sqrt(diagonal[:, None] * diagonal[None, :])]
    gather x1 -> x0, local copies, waits for them, and re-layouts: 1.94 us -> none  [shards(): diagonal = jnp.diagonal(pair_totals)]
where the time goes in v2:
time: 144 us; the launch traced here: 143 us
  Pallas kernels  140 us (97%)
  local copies, waits for them, and re-layouts  2.97 us (2%)
    pallas_call x1, Pallas kernels, shards(): pl.pallas_call(cka_kernel, out_shape=(jax.ShapeDtypeStruct((256, 2048), B...  140 us
    unnamed x4, local copies, waits for them, and re-layouts  2.97 us

profile of v2, /device:TPU:1, one launch (start us, length us, event | category | flops | bytes accessed | tf_op | source)
XLA Modules:
  0.0 143.4 jit_solution(2421516509181834149)
XLA Ops:
  0.6 139.8 %cka.1 = (bf16[256,2048]{1,0:T(8,128)(2,1)}, f32[128,128]{1,0:T(8,128)}) custom-call(bf16[32,2048]{1,0:T(8,128)(2,1)} %x_hbm.1, f32[1,2048]{1,0:T(1,128)} %bitcast.1, bf16[192,2048]{1,0:T(8,128)(2,1)} %gate_hbm.1, bf16[192,2048]{1,0:T(8,128)(2,1)} %up_hbm.1, bf16[192,2048]{1,0:T(8,128)(2,1)} %down_hbm.1, f32[1,256]{1,0:T(1,128)} %route_ref.1), custom_call_target="tpu_custom_call" | custom-call | tf_op jit(solution)/shard_map/cka/pallas_call | solution.py:473
  140.4 0.0 copy-start
  140.4 2.3 %copy.10 = bf16[256,2048]{1,0:T(8,128)(2,1)} copy(bf16[256,2048]{1,0:T(8,128)(2,1)} %get-tuple-element.4) | data formatting | bytes 2097152
  142.7 0.0 copy-done
  142.7 0.6 copy.11
Async XLA Ops:
  140.4 2.3 %copy-start = (f32[128,128]{1,0:T(8,128)S(1)}, f32[128,128]{1,0:T(8,128)}, u32[]{:S(2)}) copy-start(f32[128,128]{1,0:T(8,128)} %get-tuple-element.5) | copy-start | bytes 196612

commit v3 on v2

--- a/solution.py
+++ b/solution.py
@@ -7,10 +7,13 @@
 from jax.experimental.pallas import tpu as pltpu
 from jax.sharding import PartitionSpec as P
 
+CUTS = (0, 512, 1536, 2048)
 F32 = jnp.float32
 BF16 = jnp.bfloat16
 NT = (((1,), (1,)), ((), ()))
 MESH = pl.DeviceIdType.MESH
+FAR_FIRST = sorted(range(1, 16), key=lambda s: -min(s, 16 - s))
+TOK_FAR_FIRST = sorted(range(1, 32), key=lambda s: -min(s % 16, 16 - s % 16))
 VM = pl.BlockSpec(memory_space=pltpu.VMEM)
 
 
@@ -60,9 +63,9 @@
 def cka_kernel(
     x_hbm, gain_ref, gate_hbm, up_hbm, down_hbm, route_ref,
     out_ref, cka_ref,
-    x_ref, gate_ref, up_ref, down_ref, wide_route, nrm, tok, hid, downs, routes,
+    x_ref, gate_ref, up_ref, down_ref, wide_route, nrm, tok, gate_sum, up_sum, hid, downs, routes,
     feats, column_sum, proj_column, proj_row, cen, mid, arr, folded, part, first, mine, second, rows_sum, total_ref,
-    l_sem, z_send, z_recv, y_send, y_recv, x_send, x_recv, c_send, c_recv, w_send, w_recv, d_send, d_recv,
+    l_sem, z_send, z_recv, h_send, h_recv, y_send, y_recv, x_send, x_recv, c_send, c_recv, w_send, w_recv, d_send, d_recv,
     f_send, f_recv, a_send, a_recv, b_send, b_recv, k_sem, p_send, p_recv, s_send, s_recv, t_send, t_recv,
 ):
     me = Place()
@@ -126,7 +129,7 @@
         copy.start()
         sends.append(copy)
 
-    for s in range(1, 16):
+    for s in FAR_FIRST:
         start(push(nrm.at[:, columns], tok.at[rows, columns], z_send.at[s], z_recv.at[s], me.at_z(s)))
     for s in range(1, 16):
         source = pl.ds(pl.multiple_of((me.xh * 16 + (me.z + 16 - s) % 16) * 32, 32), 32)
@@ -137,28 +140,42 @@
         row = pl.multiple_of((x // 2) * 512, 512)
         return row, pl.multiple_of((me.c * 8 + (x % 2) * 4 + y) * 128, 128)
 
-    def y_copy(part, direction, source_step, slot):
-        row, col = spot(0, (me.y + source_step) % 4)
+    def y_copy(half, part, direction, source_step, slot):
+        row, col = spot(2 * half, (me.y + source_step) % 4)
         start_row, count = ((0, 512), (0, 256), (256, 256))[part]
         block = tok.at[pl.ds(row + start_row, count), pl.ds(col, 128)]
-        return push(block, block, y_send.at[slot], y_recv.at[slot], me.at_y(direction))
+        return push(block, block, y_send.at[half, slot], y_recv.at[half, slot], me.at_y(direction))
 
     def x_copy(slot, direction, source_step, y):
         row, col = spot(source_step, y)
         block = tok.at[pl.ds(row, 512), pl.ds(col, 128)]
         return push(block, block, x_send.at[slot, y], x_recv.at[slot, y], me.at_x(direction))
 
-    def core_copy(step_x, core):
+    def both_x(step_y):
+        y = (me.y + step_y) % 4
+        start(x_copy(0, 1, 0, y))
+        start(x_copy(1, 3, 0, y))
+
+    def core_block(step_x, core):
         x = (me.xh * 2 + me.xl + step_x) % 4
         row = pl.multiple_of((x // 2) * 512, 512)
         col = pl.multiple_of((core * 8 + (x % 2) * 4) * 128, 128)
         block = tok.at[pl.ds(row, 512), pl.ds(col, 512)]
-        return push(block, block, c_send.at[step_x], c_recv.at[step_x], me.at_core())
-
-    start(y_copy(0, 1, 0, 0))
-    start(y_copy(0, 3, 0, 1))
-    start(x_copy(0, 1, 0, me.y))
-    start(x_copy(1, 3, 0, me.y))
+        return push(block, block, c_send.at[step_x, 0], c_recv.at[step_x, 0], me.at_core())
+
+    def core_piece(step_x, y, core):
+        x = (me.xh * 2 + me.xl + step_x) % 4
+        row = pl.multiple_of((x // 2) * 512, 512)
+        col = pl.multiple_of((core * 8 + (x % 2) * 4 + y) * 128, 128)
+        block = tok.at[pl.ds(row, 512), pl.ds(col, 128)]
+        return push(block, block, c_send.at[step_x, y], c_recv.at[step_x, y], me.at_core())
+
+    row, col = spot(0, me.y)
+    own = tok.at[pl.ds(row, 512), pl.ds(col, 128)]
+    start(push(own, own, h_send, h_recv, me.at_x(2)))
+    start(y_copy(0, 0, 1, 0, 0))
+    start(y_copy(0, 0, 3, 0, 1))
+    both_x(0)
 
     owner = (me.g, me.owner)
     slot = (me.rank + 3) % 4
@@ -170,28 +187,40 @@
         down_copy.start()
         route_copy.start()
 
-    y_copy(0, 1, 3, 0).wait_recv()
-    start(y_copy(1, 1, 3, 2))
-    start(x_copy(0, 1, 0, (me.y + 3) % 4))
-    start(x_copy(1, 3, 0, (me.y + 3) % 4))
-    y_copy(0, 3, 1, 1).wait_recv()
-    start(y_copy(2, 3, 1, 3))
-    start(x_copy(0, 1, 0, (me.y + 1) % 4))
-    start(x_copy(1, 3, 0, (me.y + 1) % 4))
-    y_copy(1, 1, 2, 2).wait_recv()
-    y_copy(2, 3, 2, 3).wait_recv()
-    start(x_copy(0, 1, 0, (me.y + 2) % 4))
-    start(x_copy(1, 3, 0, (me.y + 2) % 4))
-    start(core_copy(0, me.c))
-
-    for d in (0, 3, 1, 2):
-        y = (me.y + d) % 4
-        x_copy(0, 1, 3, y).wait_recv()
-        x_copy(1, 3, 1, y).wait_recv()
-        source = 3 - 2 * (y // 2)
-        start(x_copy(2, 4 - source, source, y))
-    start(core_copy(1, me.c))
-    start(core_copy(3, me.c))
+    y_copy(0, 0, 1, 3, 0).wait_recv()
+    start(y_copy(0, 1, 1, 3, 2))
+    both_x(3)
+    y_copy(0, 0, 3, 1, 1).wait_recv()
+    start(y_copy(0, 2, 3, 1, 3))
+    both_x(1)
+    row, col = spot(2, me.y)
+    other = tok.at[pl.ds(row, 512), pl.ds(col, 128)]
+    push(other, other, h_send, h_recv, me.at_x(2)).wait_recv()
+    start(y_copy(1, 0, 1, 0, 0))
+    start(y_copy(1, 0, 3, 0, 1))
+    y_copy(0, 1, 1, 2, 2).wait_recv()
+    y_copy(0, 2, 3, 2, 3).wait_recv()
+    both_x(2)
+    start(core_block(0, me.c))
+    y_copy(1, 0, 1, 3, 0).wait_recv()
+    start(y_copy(1, 1, 1, 3, 2))
+    y_copy(1, 0, 3, 1, 1).wait_recv()
+    start(y_copy(1, 2, 3, 1, 3))
+    y_copy(1, 1, 1, 2, 2).wait_recv()
+    y_copy(1, 2, 3, 2, 3).wait_recv()
+    start(core_block(2, me.c))
+
+    def accumulate(step_x, core, first):
+        x = (me.xh * 2 + me.xl + step_x) % 4
+        cols = pl.ds(pl.multiple_of((core * 8 + (x % 2) * 4) * 128, 128), 512)
+
+        @pl.loop(0, 2)
+        def _(i):
+            chunk = pl.ds(pl.multiple_of((x // 2) * 512 + i * 256, 256), 256)
+            block = tok[chunk, cols]
+            for weight_ref, sums in ((gate_ref, gate_sum), (up_ref, up_sum)):
+                product = lax.dot_general(block, weight_ref[:, cols], NT, preferred_element_type=F32)
+                sums[chunk, :] = product if first else sums[chunk, :] + product
 
     def chunk_rows(k):
         block = (me.xh * 2 + k) % 4
@@ -205,49 +234,76 @@
 
     def make_hidden(k):
         _, rows_k = chunk_rows(k)
-        block = tok[rows_k, :]
-        gate = lax.dot_general(block, gate_ref[...], NT, preferred_element_type=F32)
-        upward = lax.dot_general(block, up_ref[...], NT, preferred_element_type=F32)
-        hid[0, rows_k, :] = (gate / (1.0 + jnp.exp(-gate)) * upward).astype(BF16)
+        gate = gate_sum[rows_k, :]
+        hid[0, rows_k, :] = (gate / (1.0 + jnp.exp(-gate)) * up_sum[rows_k, :]).astype(BF16)
 
         @pl.when(not_owner)
         def _():
             hidden_copy(k, me.rank).start()
 
+    def along_x(d):
+        y = (me.y + d) % 4
+        x_copy(0, 1, 3, y).wait_recv()
+        start(core_piece(3, y, me.c))
+        x_copy(1, 3, 1, y).wait_recv()
+        start(core_piece(1, y, me.c))
+
+    peer = 1 - me.c
+    near, far = 1 + 2 * me.xl, 3 - 2 * me.xl
     loads[2].wait()
     loads[3].wait()
-    core_copy(0, 1 - me.c).wait_recv()
-    core_copy(1 + 2 * me.xl, 1 - me.c).wait_recv()
+    accumulate(0, me.c, True)
+    along_x(0)
+    core_block(0, peer).wait_recv()
+    accumulate(0, peer, False)
+    along_x(3)
+    accumulate(2, me.c, True)
+    core_block(2, peer).wait_recv()
+    along_x(1)
+    accumulate(2, peer, False)
+    along_x(2)
+    accumulate(near, me.c, False)
+    for d in (0, 3, 1, 2):
+        core_piece(near, (me.y + d) % 4, peer).wait_recv()
+    accumulate(near, peer, False)
 
     @pl.loop(0, 2)
     def _(k):
         make_hidden(k)
 
+    accumulate(far, me.c, False)
     for d in (0, 3, 1, 2):
-        y = (me.y + d) % 4
-        x_copy(2, 1, 2, y).wait_recv()
-    start(core_copy(2, me.c))
-    core_copy(3 - 2 * me.xl, 1 - me.c).wait_recv()
-    core_copy(2, 1 - me.c).wait_recv()
+        core_piece(far, (me.y + d) % 4, peer).wait_recv()
+    accumulate(far, peer, False)
 
     @pl.loop(2, 4)
     def _(k):
         make_hidden(k)
 
-    def feature_copy(k):
+    def feature_copy(k, part):
         block, rows_k = chunk_rows(k)
-        return block, push(feats.at[rows_k, :], out_ref, f_send.at[k], f_recv, (me.g, me.base + block))
-
-    def ship(k):
-        block, copy = feature_copy(k)
+        cols = slice(CUTS[part], CUTS[part + 1])
+        device = (me.g, me.base + block)
+        return block, push(feats.at[rows_k, cols], out_ref.at[:, cols], f_send.at[part, k], f_recv, device)
+
+    def ship(k, part):
+        block, copy = feature_copy(k, part)
 
         @pl.when(block != me.q)
         def _():
             copy.start()
 
-    def first_copy(g_to, g_from, step, device):
-        src = cen.at[pl.ds(pl.multiple_of(g_to * 16, 16), 16), :]
-        return push(src, mid.at[g_from], a_send.at[step], a_recv.at[step], device)
+    def first_copy(batch, g_to, g_from, step, device):
+        cols = slice(1280 * batch, 1280 * batch + 1280)
+        src = cen.at[pl.ds(pl.multiple_of(g_to * 16, 16), 16), cols]
+        return push(src, mid.at[g_from, :, cols], a_send.at[batch, step], a_recv.at[batch, step], device)
+
+    def first_step(batch):
+        cols = slice(1280 * batch, 1280 * batch + 1280)
+        mid[me.g, :, cols] = cen[pl.ds(pl.multiple_of(me.g * 16, 16), 16), cols]
+        for s in range(1, 16):
+            g, device = owner_in_grp(s)
+            first_copy(batch, g, me.g, s, device).start()
 
     def slot_of(h):
         return (
@@ -262,13 +318,20 @@
         block = arr.at[pl.ds(0, 128), :]
         return push(block, block, b_send.at[step], b_recv.at[step], device)
 
-    def send_on(g):
-        for s in range(1, 8):
+    def send_on(batch, g):
+        for s in (2, 6, 1, 3, 5, 7, 4):
             h, device = owner_in_tok(s)
             r, k = slot_of(h)
-            push(mid.at[g, r, k], landing(g, me.h), b_send.at[s], b_recv.at[s], device).start()
+
+            @pl.when((h % 4) // 2 == batch)
+            def _():
+                push(mid.at[g, r, k], landing(g, me.h), b_send.at[s], b_recv.at[s], device).start()
+
         r, k = slot_of(me.h)
-        pltpu.make_async_copy(mid.at[g, r, k], landing(g, me.h), k_sem).start()
+
+        @pl.when((me.h % 4) // 2 == batch)
+        def _():
+            pltpu.make_async_copy(mid.at[g, r, k], landing(g, me.h), k_sem).start()
 
     def part_copy(step):
         g, device = owner_in_grp(step)
@@ -295,10 +358,6 @@
             for j in range(1, 4):
                 hidden_copy(k, j).wait_recv()
 
-            @pl.when(k > 0)
-            def _():
-                ship(k - 1)
-
             route = routes[block]
             route_column = jnp.transpose(jnp.concatenate([route] * 16, axis=0))
 
@@ -313,6 +372,8 @@
                 feats[rows_k, cols] = rounded
                 column_sum[:, cols] += jnp.sum(rounded.astype(F32).reshape(32, 8, 512), axis=0)
 
+        for k in range(3):
+            ship(k, 0)
         mean = jnp.sum(column_sum[...], axis=0, keepdims=True) / 1024
         mean_square = jnp.sum(mean * mean, axis=1, keepdims=True)
         column_sum[...] = jnp.broadcast_to(mean, (8, 2048))
@@ -328,10 +389,9 @@
             proj_column[rows_i, :] = projection
             proj_row[:, rows_i] = jnp.transpose(projection)[0:8, :]
 
-        ship(3)
-
-        @pl.loop(0, 10)
-        def _(p):
+        ship(3, 0)
+
+        def gram_block(p):
             i = p % 4
             j = (i + p // 4) % 4
             rows_i = pl.ds(pl.multiple_of(i * 256, 256), 256)
@@ -341,18 +401,20 @@
             block = gram - jnp.concatenate([column, column], axis=1) - proj_row[0:1, rows_j] + mean_square
             cen[:, pl.ds(pl.multiple_of(p * 256, 256), 256)] = block.astype(BF16)
 
-        mid[me.g] = cen[pl.ds(pl.multiple_of(me.g * 16, 16), 16), :]
-        for s in range(1, 16):
-            g, device = owner_in_grp(s)
-            first_copy(g, me.g, s, device).start()
-        send_on(me.g)
-
-        @pl.loop(1, 16)
-        def _(s):
-            g, device = owner_in_grp(16 - s)
-            first_copy(me.g, g, s, device).wait_recv()
-            send_on(g)
-
+        for batch in (0, 1):
+            pl.loop(5 * batch, 5 * batch + 5)(gram_block)
+            first_step(batch)
+
+        for batch in (0, 1):
+            send_on(batch, me.g)
+
+            @pl.loop(1, 16)
+            def _(s):
+                g, device = owner_in_grp(16 - s)
+                first_copy(batch, me.g, g, s, device).wait_recv()
+                send_on(batch, g)
+
+        out_ref[...] = feats[pl.ds(pl.multiple_of(me.q * 256, 256), 256), :]
         whole = arr.at[pl.ds(0, 128), :]
         pltpu.make_async_copy(whole, whole, k_sem).wait()
         for s in range(1, 8):
@@ -363,30 +425,34 @@
         lane = lax.broadcasted_iota(jnp.int32, (256, 256), 1) % 8
         sublane = lax.broadcasted_iota(jnp.int32, (256, 256), 0) % 8
 
-        @pl.loop(0, 4)
-        def _(i):
-            rows_i = pl.ds(pl.multiple_of(i * 256, 256), 256)
-            left = (arr[rows_i, :].astype(F32) * weight).astype(BF16)
-
-            @pl.loop(0, 4)
+        pick = lax.broadcasted_iota(jnp.int32, (1024, 128), 0) // 8
+        pick = (pick == lax.broadcasted_iota(jnp.int32, (1024, 128), 1)).astype(F32).astype(BF16)
+        folded[...] = jnp.zeros_like(folded)
+        for k in range(4):
+            ship(k, 1)
+        for i in range(4):
+            left = (arr[256 * i : 256 * i + 256, :].astype(F32) * weight).astype(BF16)
+
+            @pl.loop(i, 4)
             def _(j):
                 rows_j = pl.ds(pl.multiple_of(j * 256, 256), 256)
                 block = lax.dot_general(left, arr[rows_j, :], NT, preferred_element_type=F32)
                 block = jnp.where(lane == sublane, block, 0.0)
-                folded[pl.ds(pl.multiple_of(i * 32, 32), 32), rows_j] = jnp.sum(block.reshape(32, 8, 256), axis=1)
-
-        pick = lax.broadcasted_iota(jnp.int32, (1024, 128), 0) // 8
-        pick = (pick == lax.broadcasted_iota(jnp.int32, (1024, 128), 1)).astype(F32).astype(BF16)
-        rest = folded[...]
-        result = jnp.zeros((128, 128), F32)
-        for _ in range(3):
-            top = rest.astype(BF16)
-            rest = rest - top.astype(F32)
-            result += jnp.dot(top, pick, preferred_element_type=F32)
-        part[...] = result
-
-        for s in range(1, 16):
-            part_copy(s).start()
+                folded[32 * i : 32 * i + 32, rows_j] = jnp.sum(block.reshape(32, 8, 256), axis=1)
+
+            rest = folded[32 * i : 32 * i + 32, :]
+            result = jnp.zeros((32, 128), F32)
+            for _ in range(3):
+                top = rest.astype(BF16)
+                rest = rest - top.astype(F32)
+                result += jnp.dot(top, pick, preferred_element_type=F32)
+            part[32 * i : 32 * i + 32, :] = result
+            for g in range(4 * i, 4 * i + 4):
+
+                @pl.when(me.g != g)
+                def _():
+                    part_copy((g + 16 - me.g) % 16).start()
+
         own = part[pl.ds(pl.multiple_of(me.g * 8, 8), 8), :]
         for s in range(1, 16):
             part_copy(s).wait_recv()
@@ -394,9 +460,10 @@
         mine[...] = own
         second[me.h] = own
 
-        @pl.loop(1, 32)
-        def _(s):
+        for s in TOK_FAR_FIRST:
             row_copy(s).start()
+        for k in range(4):
+            ship(k, 2)
 
     for h in range(8):
         source = (me.g, h * 4 + me.owner_q)
@@ -421,7 +488,10 @@
         total_copy(s, (me.g + 16 - s) % 16).wait_recv()
 
     pairs = total_ref[...]
-    eye = lax.broadcasted_iota(jnp.int32, (128, 128), 0) == lax.broadcasted_iota(jnp.int32, (128, 128), 1)
+    row = lax.broadcasted_iota(jnp.int32, (128, 128), 0)
+    col = lax.broadcasted_iota(jnp.int32, (128, 128), 1)
+    pairs = jnp.where(row // 32 <= col // 32, pairs, jnp.transpose(pairs))
+    eye = row == col
     only = jnp.where(eye, pairs, 0.0)
     down = jnp.sum(only, axis=1, keepdims=True)
     across = jnp.sum(only, axis=0, keepdims=True)
@@ -432,10 +502,10 @@
 
     @pl.when(is_owner)
     def _():
-        out_ref[...] = feats[pl.ds(pl.multiple_of(me.q * 256, 256), 256), :]
         for s in range(1, 16):
             g, device = owner_in_grp(s)
-            first_copy(g, me.g, s, device).wait_send()
+            for batch in (0, 1):
+                first_copy(batch, g, me.g, s, device).wait_send()
             part_copy(s).wait_send()
         for s in range(1, 8):
             many(s, owner_in_tok(s)[1]).wait_send()
@@ -444,13 +514,13 @@
         def _(s):
             row_copy(s).wait_send()
 
-        @pl.loop(0, 4)
-        def _(k):
-            block, copy = feature_copy(k)
-
-            @pl.when(block != me.q)
-            def _():
-                copy.wait_send()
+        for k in range(4):
+            for part in range(3):
+                block, copy = feature_copy(k, part)
+
+                @pl.when(block != me.q)
+                def _():
+                    copy.wait_send()
 
     @pl.when(not_owner)
     def _():
@@ -461,7 +531,7 @@
         def _(k):
             hidden_copy(k, me.rank).wait_send()
 
-        push(feats.at[pl.ds(0, 256), :], out_ref, f_send.at[0], f_recv, owner).wait_recv()
+        push(feats.at[pl.ds(0, 256), :], out_ref, f_send.at[0, 0], f_recv, owner).wait_recv()
 
     for copy in sends:
         copy.wait_send()
@@ -486,6 +556,8 @@
             pltpu.VMEM((8, 256), F32),
             pltpu.VMEM((32, 2048), BF16),
             pltpu.VMEM((1024, 2048), BF16),
+            pltpu.VMEM((1024, 192), F32),
+            pltpu.VMEM((1024, 192), F32),
             pltpu.VMEM((4, 1024, 192), BF16),
             pltpu.VMEM((3, 192, 2048), BF16),
             pltpu.VMEM((4, 8, 256), F32),
@@ -503,9 +575,9 @@
             pltpu.VMEM((8, 8, 128), F32),
             pltpu.VMEM((8, 128), F32),
             pltpu.VMEM((128, 128), F32),
-            dma((4,)), dma((16,)), dma((16,)), dma((4,)), dma((4,)), dma((3, 4)), dma((3, 4)),
-            dma((4,)), dma((4,)), dma((2,)), dma((3, 2)), dma((4,)), dma((4, 4)),
-            dma((4,)), dma, dma((16,)), dma((16,)), dma((8,)), dma((8,)), dma,
+            dma((4,)), dma((16,)), dma((16,)), dma, dma, dma((2, 4)), dma((2, 4)), dma((2, 4)), dma((2, 4)),
+            dma((4, 4)), dma((4, 4)), dma((2,)), dma((3, 2)), dma((4,)), dma((4, 4)),
+            dma((3, 4)), dma, dma((2, 16)), dma((2, 16)), dma((8,)), dma((8,)), dma,
             dma((16,)), dma((16,)), dma((32,)), dma((8,)), dma((16,)), dma((16,)),
         ],
         compiler_params=pltpu.CompilerParams(

time: 144 us -> 134 us (0.931)
  Pallas kernels: 140 us -> 131 us
    pallas_call x1, Pallas kernels: 140 us -> 131 us  [shards(): pl.pallas_call(cka_kernel, out_shape=(jax.ShapeDtypeStruct((256, 2048), B...]
where the time goes in v3:
time: 134 us
  Pallas kernels  131 us (98%)
  local copies, waits for them, and re-layouts  2.97 us (2%)
    pallas_call x1, Pallas kernels, shards(): pl.pallas_call(cka_kernel, out_shape=(jax.ShapeDtypeStruct((256, 2048), B...  131 us
    unnamed x4, local copies, waits for them, and re-layouts  2.97 us

profile of v3, /device:TPU:1, one launch (start us, length us, event | category | flops | bytes accessed | tf_op | source)
XLA Modules:
  0.0 134.2 jit_solution(3842436722459251530)
XLA Ops:
  0.6 130.6 %cka.1 = (bf16[256,2048]{1,0:T(8,128)(2,1)}, f32[128,128]{1,0:T(8,128)}) custom-call(bf16[32,2048]{1,0:T(8,128)(2,1)} %x_hbm.1, f32[1,2048]{1,0:T(1,128)} %bitcast.1, bf16[192,2048]{1,0:T(8,128)(2,1)} %gate_hbm.1, bf16[192,2048]{1,0:T(8,128)(2,1)} %up_hbm.1, bf16[192,2048]{1,0:T(8,128)(2,1)} %down_hbm.1, f32[1,256]{1,0:T(1,128)} %route_ref.1), custom_call_target="tpu_custom_call" | custom-call | tf_op jit(solution)/shard_map/cka/pallas_call | solution.py:543
  131.3 0.0 copy-start
  131.3 2.3 %copy.10 = bf16[256,2048]{1,0:T(8,128)(2,1)} copy(bf16[256,2048]{1,0:T(8,128)(2,1)} %get-tuple-element.4) | data formatting | bytes 2097152
  133.6 0.0 copy-done
  133.6 0.6 copy.11
Async XLA Ops:
  131.3 2.3 %copy-start = (f32[128,128]{1,0:T(8,128)S(1)}, f32[128,128]{1,0:T(8,128)}, u32[]{:S(2)}) copy-start(f32[128,128]{1,0:T(8,128)} %get-tuple-element.5) | copy-start | bytes 196612

commit v4 on v3

--- a/solution.py
+++ b/solution.py
@@ -7,7 +7,7 @@
 from jax.experimental.pallas import tpu as pltpu
 from jax.sharding import PartitionSpec as P
 
-CUTS = (0, 512, 1536, 2048)
+CUTS = (0, 256, 640, 1024, 2048)
 F32 = jnp.float32
 BF16 = jnp.bfloat16
 NT = (((1,), (1,)), ((), ()))
@@ -61,9 +61,9 @@
 
 
 def cka_kernel(
-    x_hbm, gain_ref, gate_hbm, up_hbm, down_hbm, route_ref,
+    x_hbm, gain_hbm, gate_hbm, up_hbm, down_hbm, route_hbm,
     out_ref, cka_ref,
-    x_ref, gate_ref, up_ref, down_ref, wide_route, nrm, tok, gate_sum, up_sum, hid, downs, routes,
+    x_ref, gain_ref, route_ref, gate_ref, up_ref, down_ref, wide_route, nrm, tok, hid, downs, routes,
     feats, column_sum, proj_column, proj_row, cen, mid, arr, folded, part, first, mine, second, rows_sum, total_ref,
     l_sem, z_send, z_recv, h_send, h_recv, y_send, y_recv, x_send, x_recv, c_send, c_recv, w_send, w_recv, d_send, d_recv,
     f_send, f_recv, a_send, a_recv, b_send, b_recv, k_sem, p_send, p_recv, s_send, s_recv, t_send, t_recv,
@@ -75,7 +75,10 @@
     loads = [
         pltpu.make_async_copy(src, dst, l_sem.at[i])
         for i, (src, dst) in enumerate(
-            ((x_hbm, x_ref), (down_hbm, down_ref), (gate_hbm, gate_ref), (up_hbm, up_ref))
+            (
+                (x_hbm, x_ref), (gain_hbm, gain_ref), (route_hbm, route_ref),
+                (down_hbm, down_ref), (gate_hbm, gate_ref), (up_hbm, up_ref),
+            )
         )
     ]
     for load in loads:
@@ -104,7 +107,8 @@
         for s in range(1, 16, 2):
             pl.semaphore_signal(barrier, inc=1, device_id=owner_in_grp(s)[1], device_id_type=MESH)
 
-    loads[0].wait()
+    for load in loads[:3]:
+        load.wait()
     states = x_ref[...].astype(F32)
     scale = lax.rsqrt(jnp.mean(states * states, axis=1, keepdims=True) + 1e-06)
     nrm[...] = (states * scale * gain_ref[...]).astype(BF16)
@@ -113,7 +117,7 @@
     rows = pl.ds(pl.multiple_of(me.t * 32, 32), 32)
     columns = pl.ds(pl.multiple_of(group * 128, 128), 128)
     tok[rows, columns] = nrm[:, columns]
-    loads[1].wait()
+    loads[3].wait()
 
     @pl.when(is_owner)
     def _():
@@ -210,18 +214,6 @@
     y_copy(1, 2, 3, 2, 3).wait_recv()
     start(core_block(2, me.c))
 
-    def accumulate(step_x, core, first):
-        x = (me.xh * 2 + me.xl + step_x) % 4
-        cols = pl.ds(pl.multiple_of((core * 8 + (x % 2) * 4) * 128, 128), 512)
-
-        @pl.loop(0, 2)
-        def _(i):
-            chunk = pl.ds(pl.multiple_of((x // 2) * 512 + i * 256, 256), 256)
-            block = tok[chunk, cols]
-            for weight_ref, sums in ((gate_ref, gate_sum), (up_ref, up_sum)):
-                product = lax.dot_general(block, weight_ref[:, cols], NT, preferred_element_type=F32)
-                sums[chunk, :] = product if first else sums[chunk, :] + product
-
     def chunk_rows(k):
         block = (me.xh * 2 + k) % 4
         return block, pl.ds(pl.multiple_of(block * 256, 256), 256)
@@ -232,14 +224,17 @@
             hid.at[0, rows_k], hid.at[source_slot, rows_k], d_send.at[k], d_recv.at[source_slot, k], owner
         )
 
-    def make_hidden(k):
-        _, rows_k = chunk_rows(k)
-        gate = gate_sum[rows_k, :]
-        hid[0, rows_k, :] = (gate / (1.0 + jnp.exp(-gate)) * up_sum[rows_k, :]).astype(BF16)
+    def make_hidden(half):
+        half_rows = pl.ds(pl.multiple_of(((me.xh + half) % 2) * 512, 512), 512)
+        block = tok[half_rows, :]
+        gate = lax.dot_general(block, gate_ref[...], NT, preferred_element_type=F32)
+        upward = lax.dot_general(block, up_ref[...], NT, preferred_element_type=F32)
+        hid[0, half_rows, :] = (gate / (1.0 + jnp.exp(-gate)) * upward).astype(BF16)
 
         @pl.when(not_owner)
         def _():
-            hidden_copy(k, me.rank).start()
+            for k in (2 * half, 2 * half + 1):
+                hidden_copy(k, me.rank).start()
 
     def along_x(d):
         y = (me.y + d) % 4
@@ -248,37 +243,15 @@
         x_copy(1, 3, 1, y).wait_recv()
         start(core_piece(1, y, me.c))
 
-    peer = 1 - me.c
-    near, far = 1 + 2 * me.xl, 3 - 2 * me.xl
-    loads[2].wait()
-    loads[3].wait()
-    accumulate(0, me.c, True)
-    along_x(0)
-    core_block(0, peer).wait_recv()
-    accumulate(0, peer, False)
-    along_x(3)
-    accumulate(2, me.c, True)
-    core_block(2, peer).wait_recv()
-    along_x(1)
-    accumulate(2, peer, False)
-    along_x(2)
-    accumulate(near, me.c, False)
     for d in (0, 3, 1, 2):
-        core_piece(near, (me.y + d) % 4, peer).wait_recv()
-    accumulate(near, peer, False)
-
-    @pl.loop(0, 2)
-    def _(k):
-        make_hidden(k)
-
-    accumulate(far, me.c, False)
-    for d in (0, 3, 1, 2):
-        core_piece(far, (me.y + d) % 4, peer).wait_recv()
-    accumulate(far, peer, False)
-
-    @pl.loop(2, 4)
-    def _(k):
-        make_hidden(k)
+        along_x(d)
+    loads[4].wait()
+    loads[5].wait()
+    for half, twin in ((0, 1 + 2 * me.xl), (1, 3 - 2 * me.xl)):
+        core_block(2 * half, 1 - me.c).wait_recv()
+        for d in (0, 3, 1, 2):
+            core_piece(twin, (me.y + d) % 4, 1 - me.c).wait_recv()
+        make_hidden(half)
 
     def feature_copy(k, part):
         block, rows_k = chunk_rows(k)
@@ -453,6 +426,8 @@
                 def _():
                     part_copy((g + 16 - me.g) % 16).start()
 
+        for k in range(4):
+            ship(k, 2)
         own = part[pl.ds(pl.multiple_of(me.g * 8, 8), 8), :]
         for s in range(1, 16):
             part_copy(s).wait_recv()
@@ -463,7 +438,7 @@
         for s in TOK_FAR_FIRST:
             row_copy(s).start()
         for k in range(4):
-            ship(k, 2)
+            ship(k, 3)
 
     for h in range(8):
         source = (me.g, h * 4 + me.owner_q)
@@ -515,7 +490,7 @@
             row_copy(s).wait_send()
 
         for k in range(4):
-            for part in range(3):
+            for part in range(4):
                 block, copy = feature_copy(k, part)
 
                 @pl.when(block != me.q)
@@ -539,25 +514,25 @@
 
 def shards(probe_states, norm_gain, gate_weight, up_weight, down_weight, route_weight):
     dma = pltpu.SemaphoreType.DMA
-    hbm = pl.BlockSpec(memory_space=pl.ANY)
+    hbm = pl.BlockSpec(memory_space=pltpu.HBM)
     return pl.pallas_call(
         cka_kernel,
         out_shape=(
             jax.ShapeDtypeStruct((256, 2048), BF16),
             jax.ShapeDtypeStruct((128, 128), F32),
         ),
-        in_specs=[hbm, VM, hbm, hbm, hbm, VM],
+        in_specs=[hbm] * 6,
         out_specs=(VM, VM),
         scratch_shapes=[
             pltpu.VMEM((32, 2048), BF16),
+            pltpu.VMEM((1, 2048), F32),
+            pltpu.VMEM((1, 256), F32),
             pltpu.VMEM((192, 2048), BF16),
             pltpu.VMEM((192, 2048), BF16),
             pltpu.VMEM((192, 2048), BF16),
             pltpu.VMEM((8, 256), F32),
             pltpu.VMEM((32, 2048), BF16),
             pltpu.VMEM((1024, 2048), BF16),
-            pltpu.VMEM((1024, 192), F32),
-            pltpu.VMEM((1024, 192), F32),
             pltpu.VMEM((4, 1024, 192), BF16),
             pltpu.VMEM((3, 192, 2048), BF16),
             pltpu.VMEM((4, 8, 256), F32),
@@ -575,9 +550,9 @@
             pltpu.VMEM((8, 8, 128), F32),
             pltpu.VMEM((8, 128), F32),
             pltpu.VMEM((128, 128), F32),
-            dma((4,)), dma((16,)), dma((16,)), dma, dma, dma((2, 4)), dma((2, 4)), dma((2, 4)), dma((2, 4)),
+            dma((6,)), dma((16,)), dma((16,)), dma, dma, dma((2, 4)), dma((2, 4)), dma((2, 4)), dma((2, 4)),
             dma((4, 4)), dma((4, 4)), dma((2,)), dma((3, 2)), dma((4,)), dma((4, 4)),
-            dma((3, 4)), dma, dma((2, 16)), dma((2, 16)), dma((8,)), dma((8,)), dma,
+            dma((4, 4)), dma, dma((2, 16)), dma((2, 16)), dma((8,)), dma((8,)), dma,
             dma((16,)), dma((16,)), dma((32,)), dma((8,)), dma((16,)), dma((16,)),
         ],
         compiler_params=pltpu.CompilerParams(

time: 134 us -> 125 us (0.933)
  Pallas kernels: 131 us -> 121 us
    pallas_call x1, Pallas kernels: 131 us -> 121 us  [shards(): pl.pallas_call(cka_kernel, out_shape=(jax.ShapeDtypeStruct((256, 2048), B...]
where the time goes in v4:
time: 125 us
  Pallas kernels  121 us (97%)
  local copies, waits for them, and re-layouts  2.97 us (2%)
    pallas_call x1, Pallas kernels, shards(): pl.pallas_call(cka_kernel, out_shape=(jax.ShapeDtypeStruct((256, 2048), B...  121 us
    unnamed x4, local copies, waits for them, and re-layouts  2.97 us

profile of v4, /device:TPU:1, one launch (start us, length us, event | category | flops | bytes accessed | tf_op | source)
XLA Modules:
  0.0 124.5 jit_solution(2421279721875170634)
XLA Ops:
  0.6 120.9 %cka.1 = (bf16[256,2048]{1,0:T(8,128)(2,1)}, f32[128,128]{1,0:T(8,128)}) custom-call(bf16[32,2048]{1,0:T(8,128)(2,1)} %x_hbm.1, f32[1,2048]{1,0:T(1,128)} %bitcast.1, bf16[192,2048]{1,0:T(8,128)(2,1)} %gate_hbm.1, bf16[192,2048]{1,0:T(8,128)(2,1)} %up_hbm.1, bf16[192,2048]{1,0:T(8,128)(2,1)} %down_hbm.1, f32[1,256]{1,0:T(1,128)} %route_hbm.1), custom_call_target="tpu_custom_call" | custom-call | tf_op jit(solution)/shard_map/cka/pallas_call | solution.py:518
  121.5 0.0 copy-start
  121.5 2.3 %copy.10 = bf16[256,2048]{1,0:T(8,128)(2,1)} copy(bf16[256,2048]{1,0:T(8,128)(2,1)} %get-tuple-element.4) | data formatting | bytes 2097152
  123.9 0.0 copy-done
  123.9 0.6 copy.11
Async XLA Ops:
  121.5 2.3 %copy-start = (f32[128,128]{1,0:T(8,128)S(1)}, f32[128,128]{1,0:T(8,128)}, u32[]{:S(2)}) copy-start(f32[128,128]{1,0:T(8,128)} %get-tuple-element.5) | copy-start | bytes 196612

commit v5 on v4

--- a/solution.py
+++ b/solution.py
@@ -225,15 +225,15 @@
         )
 
     def make_hidden(half):
-        half_rows = pl.ds(pl.multiple_of(((me.xh + half) % 2) * 512, 512), 512)
-        block = tok[half_rows, :]
-        gate = lax.dot_general(block, gate_ref[...], NT, preferred_element_type=F32)
-        upward = lax.dot_general(block, up_ref[...], NT, preferred_element_type=F32)
-        hid[0, half_rows, :] = (gate / (1.0 + jnp.exp(-gate)) * upward).astype(BF16)
-
-        @pl.when(not_owner)
-        def _():
-            for k in (2 * half, 2 * half + 1):
+        for k in (2 * half, 2 * half + 1):
+            _, rows_k = chunk_rows(k)
+            block = tok[rows_k, :]
+            gate = lax.dot_general(block, gate_ref[...], NT, preferred_element_type=F32)
+            upward = lax.dot_general(block, up_ref[...], NT, preferred_element_type=F32)
+            hid[0, rows_k, :] = (gate / (1.0 + jnp.exp(-gate)) * upward).astype(BF16)
+
+            @pl.when(not_owner)
+            def _():
                 hidden_copy(k, me.rank).start()
 
     def along_x(d):

time: 125 us -> 124 us (level)
  no operation moved by 1% of the time
where the time goes in v5:
time: 124 us
  Pallas kernels  120 us (97%)
  local copies, waits for them, and re-layouts  2.97 us (2%)
    pallas_call x1, Pallas kernels, shards(): pl.pallas_call(cka_kernel, out_shape=(jax.ShapeDtypeStruct((256, 2048), B...  120 us
    unnamed x4, local copies, waits for them, and re-layouts  2.97 us

profile of v5, /device:TPU:1, one launch (start us, length us, event | category | flops | bytes accessed | tf_op | source)
XLA Modules:
  0.0 124.0 jit_solution(17747641829344128361)
XLA Ops:
  0.6 120.4 %cka.1 = (bf16[256,2048]{1,0:T(8,128)(2,1)}, f32[128,128]{1,0:T(8,128)}) custom-call(bf16[32,2048]{1,0:T(8,128)(2,1)} %x_hbm.1, f32[1,2048]{1,0:T(1,128)} %bitcast.1, bf16[192,2048]{1,0:T(8,128)(2,1)} %gate_hbm.1, bf16[192,2048]{1,0:T(8,128)(2,1)} %up_hbm.1, bf16[192,2048]{1,0:T(8,128)(2,1)} %down_hbm.1, f32[1,256]{1,0:T(1,128)} %route_hbm.1), custom_call_target="tpu_custom_call" | custom-call | tf_op jit(solution)/shard_map/cka/pallas_call | solution.py:518
  121.0 0.0 copy-start
  121.0 2.3 %copy.10 = bf16[256,2048]{1,0:T(8,128)(2,1)} copy(bf16[256,2048]{1,0:T(8,128)(2,1)} %get-tuple-element.4) | data formatting | bytes 2097152
  123.4 0.0 copy-done
  123.4 0.6 copy.11
Async XLA Ops:
  121.0 2.3 %copy-start = (f32[128,128]{1,0:T(8,128)S(1)}, f32[128,128]{1,0:T(8,128)}, u32[]{:S(2)}) copy-start(f32[128,128]{1,0:T(8,128)} %get-tuple-element.5) | copy-start | bytes 196612
